TPU v7x, 512 devices: a whole 4x8x8 slice. The times are simulated.
512 devices in a mesh: tm: 16 (over y, core), lat: 4 (over x), lon: 8 (over z).
Axes of the slice: x: 4, y: 8, z: 8, core: 2. Of those that a mesh axis runs over, the one named last changes fastest.
Arguments:
- residuals: bfloat16 [1024, 180, 1024], P('tm', 'lat', 'lon'), may hold values from -10 to 10
- diffusivity: float32 [180, 1024], P('lat', 'lon'), may hold values from 0.03 to 0.24
Outputs:
- projected: bfloat16 [1024, 180, 1024], P('tm', 'lat', 'lon')
All inputs are finite; a program needn't handle non-finite values.
Results may differ from a plain program's by a relative error of at most 0.019.
Values may be sent and summed in bfloat16 or wider, within the bound.
A program may use at most 64 MiB of HBM per device.

v0:
```python
import math

import jax
import jax.numpy as jnp
from jax import lax
from jax.sharding import PartitionSpec as P

RANK = 32
PASSES = 4
POWER = 3


exact_precision = lax.Precision.HIGHEST


def with_halo(block, sides, width, periodic):
    for axis, dim in sides:
        count = lax.axis_size(axis)
        forward = [(i, i + 1) for i in range(count - 1)]
        if periodic:
            forward.append((count - 1, 0))
        backward = [(target, source) for source, target in forward]
        low = lax.ppermute(
            lax.slice_in_dim(block, block.shape[dim] - width, None, axis=dim), axis, forward
        )
        high = lax.ppermute(lax.slice_in_dim(block, 0, width, axis=dim), axis, backward)
        block = jnp.concatenate([low, block, high], axis=dim)
    return block


def swapped(block, axis, stride):
    count = lax.axis_size(axis)
    route = []
    for low in range(count):
        high = low | 1 << stride
        if high != low and high < count:
            route += [(low, high), (high, low)]
    return lax.ppermute(block, axis, route)


def stencil(current, coeffs):
    center = current[:, 1:-1, 1:-1]
    middle = coeffs[:, 1:-1, 1:-1]
    northward = 0.5 * (middle + coeffs[:, :-2, 1:-1]) * (current[:, :-2, 1:-1] - center)
    southward = 0.5 * (middle + coeffs[:, 2:, 1:-1]) * (current[:, 2:, 1:-1] - center)
    westward = 0.5 * (middle + coeffs[:, 1:-1, :-2]) * (current[:, 1:-1, :-2] - center)
    eastward = 0.5 * (middle + coeffs[:, 1:-1, 2:]) * (current[:, 1:-1, 2:] - center)
    return center + (northward + southward + westward + eastward)


def orthonormal(block):
    inner = jnp.dot(block.T, block, precision=exact_precision)
    lower = jnp.linalg.cholesky(inner)
    return jax.scipy.linalg.solve_triangular(lower, block.T, lower=True).T


def top_space(gram):
    basis = orthonormal(gram[:, :RANK])
    for step_index in range(POWER):
        basis = orthonormal(jnp.dot(gram, basis, precision=exact_precision))
    return basis


def mode_block(stacked, gram):
    basis = top_space(gram).astype(jnp.bfloat16)
    modes = jnp.dot(basis.T, stacked, preferred_element_type=jnp.float32).astype(jnp.bfloat16)
    return (basis, modes)


def shards(residuals, diffusivity):
    snap_count, height, width = residuals.shape
    current = residuals.astype(jnp.float32)
    coeffs = diffusivity[None]
    for pass_index in range(PASSES):
        field_ext, coeff_ext = (
            with_halo(current.astype(jnp.bfloat16), (("lon", 2),), 1, True).astype(current.dtype),
            with_halo(coeffs.astype(jnp.bfloat16), (("lon", 2),), 1, True).astype(coeffs.dtype),
        )
        field_ext, coeff_ext = (
            with_halo(field_ext.astype(jnp.bfloat16), (("lat", 1),), 1, False).astype(
                field_ext.dtype
            ),
            with_halo(coeff_ext.astype(jnp.bfloat16), (("lat", 1),), 1, False).astype(
                coeff_ext.dtype
            ),
        )
        current = stencil(field_ext, coeff_ext)
    rows = (lax.axis_index("lat") * height + jnp.arange(height)).astype(jnp.float32)
    latitude = (rows + 0.5) * math.pi / (height * lax.axis_size("lat")) - math.pi / 2
    scale = jnp.sqrt(jnp.cos(latitude))
    weighted = (
        (current * scale[None, :, None]).astype(jnp.bfloat16).reshape(snap_count, height * width)
    )
    gram = lax.psum(
        jnp.dot(weighted, weighted.T, preferred_element_type=jnp.float32), ("lat", "lon")
    )
    basis, modes = mode_block(weighted, gram)
    levels_count = lax.axis_size("tm").bit_length() - 1
    for level_index in range(levels_count):
        partner = swapped(modes, "tm", level_index)
        upper_bit = lax.axis_index("tm") >> level_index & 1
        lower_first = jnp.concatenate([modes, partner], axis=0)
        upper_first = jnp.concatenate([partner, modes], axis=0)
        stacked = jnp.where(upper_bit == 0, lower_first, upper_first)
        gram = lax.psum(
            jnp.dot(stacked, stacked.T, preferred_element_type=jnp.float32), ("lat", "lon")
        )
        basis, modes = mode_block(stacked, gram)
    basis_f = basis.astype(jnp.float32)
    curvature = jnp.dot(
        basis_f.T, jnp.dot(gram, basis_f, precision=exact_precision), precision=exact_precision
    )
    factor = jnp.linalg.cholesky(curvature)
    coef = lax.psum(jnp.dot(weighted, modes.T, preferred_element_type=jnp.float32), ("lat", "lon"))
    solved = jax.scipy.linalg.cho_solve((factor, True), coef.T).T.astype(jnp.bfloat16)
    projected = jnp.dot(solved, modes, preferred_element_type=jnp.float32).astype(jnp.bfloat16)
    return projected.reshape(snap_count, height, width)


def solution(mesh):
    return jax.shard_map(
        shards,
        mesh=mesh,
        in_specs=(P("tm", "lat", "lon"), P("lat", "lon")),
        out_specs=P("tm", "lat", "lon"),
        check_vma=False,
    )
```

profile of v0, /device:TPU:24, one launch (start us, length us, event | category | flops | bytes accessed | tf_op | source)
XLA Modules:
  0.0 1146.6 jit_solution(14412167387438944083)
XLA Ops:
  0.8 4.3 collective-permute-start.4
  5.1 8.6 collective-permute-start.5
  15.7 3.4 collective-permute-start.6
  22.3 5.1 collective-permute-start.1
  29.0 4.5 collective-permute-start.2
  35.5 4.3 collective-permute-done.3
  40.5 4.0 fusion.31
  44.5 3.5 collective-permute-start.8
  48.0 3.8 collective-permute-start.9
  53.8 3.4 collective-permute-start.10
  59.1 4.3 collective-permute-done.11
  64.1 4.0 fusion.22
  68.1 3.9 collective-permute-start.12
  72.1 3.1 collective-permute-start.13
  77.8 3.1 collective-permute-start.14
  82.8 4.3 collective-permute-done.15
  87.9 4.0 fusion.13
  91.9 3.4 collective-permute-start.16
  95.3 3.6 collective-permute-start.17
  104.9 4.3 collective-permute-done.19
  109.9 4.1 fusion.4
  115.9 139.3 %psum.42 = f32[64,64]{1,0:T(8,128)S(1)} all-reduce(f32[64,64]{1,0:T(8,128)S(1)} %fusion.40), channel_id=1, replica_groups=mesh['tm'=16,'lat'=4,'lon'=8] {'lat','lon'}, use_global_device_ids=true, to_apply=%region_0.0 | all-reduce | flops 4096 | bytes 32768 | tf_op jit(solution)/shard_map/psum | solution.py:94
  255.5 2.9 cholesky.329
  262.8 2.9 cholesky.340
  270.2 2.9 cholesky.351
  277.5 2.9 cholesky.362
  288.7 137.7 %psum.43 = f32[64,64]{1,0:T(8,128)S(1)} all-reduce(f32[64,64]{1,0:T(8,128)S(1)} %fusion.51), channel_id=1, replica_groups=mesh['tm'=16,'lat'=4,'lon'=8] {'lat','lon'}, use_global_device_ids=true, to_apply=%region_3.6 | all-reduce | flops 4096 | bytes 32768 | tf_op jit(solution)/shard_map/psum | solution.py:105
  426.7 2.9 cholesky.373
  434.1 2.9 cholesky.384
  441.4 2.9 cholesky.395
  448.8 2.9 cholesky.406
  458.4 7.0 collective-permute-done.21
  465.8 137.7 %psum.44 = f32[64,64]{1,0:T(8,128)S(1)} all-reduce(f32[64,64]{1,0:T(8,128)S(1)} %fusion.50), channel_id=1, replica_groups=mesh['tm'=16,'lat'=4,'lon'=8] {'lat','lon'}, use_global_device_ids=true, to_apply=%region_4.7 | all-reduce | flops 4096 | bytes 32768 | tf_op jit(solution)/shard_map/psum | solution.py:105
  603.8 2.9 cholesky.417
  611.1 2.9 cholesky.428
  618.5 2.9 cholesky.439
  625.9 2.9 cholesky.450
  635.5 11.7 %collective-permute-done.22 = bf16[32,5760]{1,0:T(8,128)(2,1)S(1)} collective-permute-done((bf16[32,5760]{1,0:T(8,128)(2,1)S(1)}, bf16[32,5760]{1,0:T(8,128)(2,1)S(1)}, u32[]{:S(2)}, u32[]{:S(2)}) %collective-permute-start.22) | collective-permute-done | bytes 368672 | tf_op jit(solution)/shard_map/ppermute | solution.py:38
  647.6 137.7 %psum.45 = f32[64,64]{1,0:T(8,128)S(1)} all-reduce(f32[64,64]{1,0:T(8,128)S(1)} %fusion.49), channel_id=1, replica_groups=mesh['tm'=16,'lat'=4,'lon'=8] {'lat','lon'}, use_global_device_ids=true, to_apply=%region_5.8 | all-reduce | flops 4096 | bytes 32768 | tf_op jit(solution)/shard_map/psum | solution.py:105
  785.6 2.9 cholesky.461
  793.0 2.9 cholesky.472
  800.3 2.9 cholesky.483
  807.7 2.9 cholesky.494
  814.9 5.2 collective-permute-start.23
  820.0 12.0 %collective-permute-done.23 = bf16[32,5760]{1,0:T(8,128)(2,1)S(1)} collective-permute-done((bf16[32,5760]{1,0:T(8,128)(2,1)S(1)}, bf16[32,5760]{1,0:T(8,128)(2,1)S(1)}, u32[]{:S(2)}, u32[]{:S(2)}) %collective-permute-start.23) | collective-permute-done | bytes 368672 | tf_op jit(solution)/shard_map/ppermute | solution.py:38
  832.4 137.7 %psum.46 = f32[64,64]{1,0:T(8,128)S(1)} all-reduce(f32[64,64]{1,0:T(8,128)S(1)} %fusion.48), channel_id=1, replica_groups=mesh['tm'=16,'lat'=4,'lon'=8] {'lat','lon'}, use_global_device_ids=true, to_apply=%region_6.9 | all-reduce | flops 4096 | bytes 32768 | tf_op jit(solution)/shard_map/psum | solution.py:105
  970.4 2.9 cholesky.505
  1007.1 137.7 %psum.47 = f32[32,64]{1,0:T(8,128)S(1)} all-reduce(f32[32,64]{1,0:T(8,128)S(1)} %fusion.43), channel_id=1, replica_groups=mesh['tm'=16,'lat'=4,'lon'=8] {'lat','lon'}, use_global_device_ids=true, to_apply=%region_7.10 | all-reduce | flops 2048 | bytes 16384 | tf_op jit(solution)/shard_map/psum | solution.py:114
  (253 shorter events, 145.1 us)
Async XLA Ops:
  0.8 14.8 %collective-permute-start.4 = (bf16[1,45,1]{2,1,0:T(8,128)(2,1)S(1)}, bf16[1,45,1]{2,1,0:T(8,128)(2,1)S(1)}, u32[]{:S(2)}, u32[]{:S(2)}) collective-permute-start(bf16[1,45,1]{2,1,0:T(8,128)(2,1)S(1)} %get-tuple-element.29), channel_id=1, source_target_pairs={{0,1},{1,2},{2,3},{3,4},{4,5},{5,6},{6,7},{7,0},{8,9},{9,10},{10,1... | collective-permute-start | bytes 278 | tf_op jit(solution)/shard_map/ppermute | solution.py:23
  5.1 10.5 collective-permute-start.5
  15.7 11.8 %collective-permute-start.6 = (bf16[1,1,130]{2,1,0:T(2,128)(2,1)S(1)}, bf16[1,1,130]{2,1,0:T(2,128)(2,1)S(1)}, u32[]{:S(2)}, u32[]{:S(2)}) collective-permute-start(bf16[1,1,130]{2,1,0:T(2,128)(2,1)S(1)} %get-tuple-element.27), channel_id=1, source_target_pairs={{0,8},{8,16},{16,24},{1,9},{9,17},{17,25},{2,10},{10,18},{18,26},{... | collective-permute-start | bytes 788 | tf_op jit(solution)/shard_map/ppermute | solution.py:23
  19.1 8.4 collective-permute-start.7
  20.4 7.2 collective-permute-start
  22.3 6.5 collective-permute-start.1
  29.0 6.5 collective-permute-start.2
  33.6 6.2 collective-permute-start.3
  44.5 7.3 collective-permute-start.8
  48.0 5.6 collective-permute-start.9
  53.8 5.3 collective-permute-start.10
  57.2 6.2 collective-permute-start.11
  68.1 7.1 collective-permute-start.12
  72.1 5.6 collective-permute-start.13
  77.8 5.0 collective-permute-start.14
  80.9 6.2 collective-permute-start.15
  91.9 7.1 collective-permute-start.16
  95.3 5.6 collective-permute-start.17
  101.0 3.8 collective-permute-start.18
  103.0 6.2 collective-permute-start.19
  284.7 3.6 collective-permute-start.20
  456.0 9.4 collective-permute-start.21
  633.1 14.1 %collective-permute-start.22 = (bf16[32,5760]{1,0:T(8,128)(2,1)S(1)}, bf16[32,5760]{1,0:T(8,128)(2,1)S(1)}, u32[]{:S(2)}, u32[]{:S(2)}) collective-permute-start(bf16[32,5760]{1,0:T(8,128)(2,1)S(1)} %convolution_convert_fusion.3), channel_id=1, source_target_pairs={{0,128},{128,0},{32,160},{160,32},{64,192},{192,64},{96,224},{224,... | collective-permute-start | bytes 1105928 | tf_op jit(solution)/shard_map/ppermute | solution.py:38
  814.9 17.1 %collective-permute-start.23 = (bf16[32,5760]{1,0:T(8,128)(2,1)S(1)}, bf16[32,5760]{1,0:T(8,128)(2,1)S(1)}, u32[]{:S(2)}, u32[]{:S(2)}) collective-permute-start(bf16[32,5760]{1,0:T(8,128)(2,1)S(1)} %convolution_convert_fusion.2), channel_id=1, source_target_pairs={{0,256},{256,0},{32,288},{288,32},{64,320},{320,64},{96,352},{352,... | collective-permute-start | bytes 1105928 | tf_op jit(solution)/shard_map/ppermute | solution.py:38
where the time goes:
time: 1150 us
  blocking collectives  828 us (72%)
  other arithmetic  161 us (14%)
  starting transfers between devices  76.1 us (7%)
  waiting for transfers between devices  58.6 us (5%)
  matrix products  15.4 us (1%)
    psum x4, blocking collectives, shards(): lax.psum(jnp.dot(stacked, stacked.T, preferred_element_type=jnp.float32),...  551 us
    psum x1, blocking collectives, shards(): lax.psum(jnp.dot(weighted, weighted.T, preferred_element_type=jnp.float32...  139 us
    psum x1, blocking collectives, shards(): lax.psum(jnp.dot(weighted, modes.T, preferred_element_type=jnp.float32),...  138 us
    another operation x60, other arithmetic, orthonormal(): lower = jnp.linalg.cholesky(inner)  72 us
    another operation x40, other arithmetic, orthonormal(): return jax.scipy.linalg.solve_triangular(lower, block.T, lower=True).T  61.7 us
    ppermute x10, starting transfers between devices, with_halo(): lax.ppermute(lax.slice_in_dim(block, block.shape[dim] - width, None, axis...  33.4 us
    ppermute x4, waiting for transfers between devices, swapped(): return lax.ppermute(block, axis, route)  32.3 us
    ppermute x10, starting transfers between devices, with_halo(): lax.ppermute(lax.slice_in_dim(block, 0, width, axis=dim), axis, backward)  30.7 us
  transfers between devices with their start and end apart: 24, of which 16 were waited for; matrix products, arithmetic and copies ran while one was open for 0% of the time, Pallas kernels for 0%

commit v1 on v0

v1 whole, which is shorter than its diff:
```python
import functools
import math

import jax
import jax.numpy as jnp
from jax import lax
from jax.experimental import pallas as pl
from jax.experimental.pallas import tpu as pltpu
from jax.sharding import PartitionSpec as P

RANK = 32
PASSES = 4
POWER = 3
LANES = 128
HIGHEST = lax.Precision.HIGHEST
MESH = pl.DeviceIdType.MESH


def dot(a, b, dims, precision=None):
    return lax.dot_general(
        a, b, (dims, ((), ())), precision=precision, preferred_element_type=jnp.float32
    )


def matmul(a, b):
    return dot(a, b, ((1,), (0,)), HIGHEST)


def matmul_t(a, b):
    return dot(a, b, ((1,), (1,)), HIGHEST)


def rounded(a):
    return a.astype(jnp.bfloat16).astype(jnp.float32)


def factor_rows(m, start, block=8):
    count = RANK // 8
    v = [m[8 * i : 8 * i + 8] for i in range(count)]
    sub = lax.broadcasted_iota(jnp.int32, (8, LANES), 0)
    lane = lax.broadcasted_iota(jnp.int32, (8, LANES), 1)

    def column(x, j):
        return jnp.broadcast_to(x[:, start + j : start + j + 1], (8, LANES))

    for k in range(0, RANK, block):
        b, s = k // 8, k % 8
        row = [jnp.broadcast_to(v[b][s + j : s + j + 1, :], (8, LANES)) for j in range(block)]
        diag = {(i, j): column(row[i], k + j) for i in range(block) for j in range(i, block)}
        cols = [[column(v[i], k + j) for j in range(block)] for i in range(b, count)]
        inverse = []
        for i in range(block):
            inverse.append(1.0 / diag[i, i])
            ratio = {j: diag[i, j] * inverse[i] for j in range(i + 1, block)}
            for j in range(i + 1, block):
                for n in range(j, block):
                    diag[j, n] = diag[j, n] - ratio[j] * diag[i, n]
                row[j] = row[j] - ratio[j] * row[i]
                for c in cols:
                    c[j] = c[j] - c[i] * ratio[j]
        scaled = [row[i] * inverse[i] for i in range(block)]
        for i in range(b, count):
            total = None
            for j in range(block):
                if i == b and s + j == 7:
                    continue
                c = cols[i - b][j]
                if i == b:
                    c = jnp.where(sub > s + j, c, 0.0)
                term = c * scaled[j]
                total = term if total is None else total + term
            if total is not None:
                v[i] = v[i] - total
    out = []
    for i in range(count):
        pivot = jnp.sum(
            jnp.where(lane == sub + (start + 8 * i), v[i], 0.0), axis=1, keepdims=True
        )
        out.append(v[i] * lax.rsqrt(pivot))
    return jnp.concatenate(out, axis=0)


def half_mask(rows, side):
    lane = lax.broadcasted_iota(jnp.int32, (rows, LANES), 1)
    return (lane < 64) if side == 0 else (lane >= 64)


def inner_beside(p, side):
    start = 64 * (1 - side)
    parts = []
    if start:
        parts.append(jnp.zeros((start, LANES), jnp.float32))
    parts.append(p)
    parts.append(jnp.zeros((LANES - start - RANK, LANES), jnp.float32))
    return p + matmul_t(p, jnp.concatenate(parts, axis=0))


def top_rows(problems):
    row = lax.broadcasted_iota(jnp.int32, (RANK, LANES), 0)
    lane = lax.broadcasted_iota(jnp.int32, (RANK, LANES), 1)
    starts = tuple(
        jnp.where(lane == row + 64 * side, 1.0, 0.0).astype(jnp.float32) for _, side in problems
    )

    def body(_, bases):
        out = []
        for (gram, side), p in zip(problems, bases):
            keep = half_mask(RANK, side)
            p = jnp.where(keep, matmul(p, gram), 0.0)
            out.append((inner_beside(p, side), side, keep))
        return tuple(
            jnp.where(keep, factor_rows(m, 64 * (1 - side)), 0.0) for m, side, keep in out
        )

    return lax.fori_loop(0, POWER + 1, body, starts)


def merge_pairs(grams):
    problems = [(g, side) for g in grams for side in (0, 1)]
    tops = top_rows(problems)
    zeros = jnp.zeros((64, LANES), jnp.float32)
    joined = [
        jnp.concatenate([rounded(tops[2 * i]), rounded(tops[2 * i + 1]), zeros], axis=0)
        for i in range(len(grams))
    ]
    merged = [matmul_t(matmul(j, g), j) for j, g in zip(joined, grams)]
    second = top_rows([(m, 0) for m in merged])
    return [matmul(rounded(p), j) for p, j in zip(second, joined)]


def order_of(n):
    return sorted(range(1, n), key=lambda d: -min(d, n - d))


def merge_kernel(
    ny, nx, nz, y_ref, out_ref,
    pair, gram_part, gram_rs, gram_z, gram_ag,
    a_own, a_all, g2_part, g2_rs, g2_y, g2_z, g2_ag,
    f_all, coef_x, coef_z,
    send, recv,
):
    t, x, z = lax.axis_index("tm"), lax.axis_index("lat"), lax.axis_index("lon")
    y, c = t // 2, lax.rem(t, 2)
    nxc = 2 * nx
    p = x * 2 + c
    half = y_ref.shape[0] // 2
    per = half // ny

    def dev_xc(q):
        return (y * 2 + lax.rem(q, 2), q // 2, z)

    def dev_x(q):
        return (t, q, z)

    def dev_z(q):
        return (t, x, q)

    def dev_y(q):
        return (q * 2 + c, x, z)

    partner = (y * 2 + (1 - c), x, z)
    barrier = pltpu.get_barrier_semaphore()
    groups = ((nxc, p, dev_xc), (nz, z, dev_z), (ny, y, dev_y))
    for n, me, dev in groups:
        for d in range(1, n):
            pl.semaphore_signal(
                barrier, inc=1, device_id=dev(lax.rem(me + d, n)), device_id_type=MESH
            )
    pl.semaphore_wait(barrier, sum(n - 1 for n, _, _ in groups))

    pending = []
    stage_count = [0]

    def exchange(n, me, dev, source, target):
        stage = stage_count[0]
        stage_count[0] += 1
        copies = {}
        for d in order_of(n):
            q = lax.rem(me + d, n)
            copy = pltpu.make_async_remote_copy(
                src_ref=source(q), dst_ref=target,
                send_sem=send.at[stage, d], recv_sem=recv.at[stage, d],
                device_id=dev(q), device_id_type=MESH,
            )
            copy.start()
            copies[d] = copy
            pending.append(copy)
        return copies

    def arrive(copies):
        for d in sorted(copies, key=lambda d: min(d, len(copies) + 1 - d)):
            copies[d].wait_recv()

    stage = stage_count[0]
    stage_count[0] += 1
    swap = pltpu.make_async_remote_copy(
        src_ref=y_ref.at[pl.ds(half * (1 - c), half)], dst_ref=pair.at[c],
        send_sem=send.at[stage, 0], recv_sem=recv.at[stage, 0],
        device_id=partner, device_id_type=MESH,
    )
    swap.start()
    pending.append(swap)
    pair[c] = y_ref[pl.ds(half * c, half)]
    swap.wait_recv()

    def rows_of(r):
        return jnp.concatenate([pair[0, r], pair[1, r]], axis=0)

    total = jnp.zeros((LANES, LANES), jnp.float32)
    for r in range(0, half, 2):
        wide = jnp.concatenate([rows_of(r), rows_of(r + 1)], axis=1)
        total = total + dot(wide, wide, ((1,), (1,)))
    piece = LANES // nxc
    gram_part[...] = total.reshape(nxc, piece, LANES)
    copies = exchange(nxc, p, dev_xc, lambda q: gram_part.at[q], gram_rs.at[p])
    gram_rs[p] = gram_part[p]
    arrive(copies)
    gram_z[z] = jnp.sum(gram_rs[...], axis=0)
    copies = exchange(nz, z, dev_z, lambda q: gram_z.at[z], gram_z.at[z])
    arrive(copies)
    gram_ag[p] = jnp.sum(gram_z[...], axis=0)
    copies = exchange(nxc, p, dev_xc, lambda q: gram_ag.at[p], gram_ag.at[p])
    arrive(copies)
    gram = gram_ag[...].reshape(LANES, LANES)

    basis = merge_pairs([gram])[0].astype(jnp.bfloat16)

    for r in range(0, half, 2):
        wide = jnp.concatenate([rows_of(r), rows_of(r + 1)], axis=1)
        modes = dot(basis, wide, ((1,), (0,))).astype(jnp.bfloat16)
        a_own[r] = modes[:, :LANES]
        a_own[r + 1] = modes[:, LANES:]
    copies = exchange(ny, y, dev_y, lambda q: a_own.at[pl.ds(per * q, per)], a_all.at[y])
    a_all[y] = a_own[pl.ds(per * y, per)]
    arrive(copies)

    stacked = jnp.concatenate(
        [
            jnp.concatenate([a_all[b, r] for b in range(ny)], axis=0)
            for r in range(per)
        ],
        axis=1,
    )
    big = ny * RANK
    full = dot(stacked, stacked, ((1,), (1,)))
    width = full.shape[1]
    near = ny // 2
    if width % LANES:
        full = jnp.concatenate(
            [full, jnp.zeros((big, LANES - width % LANES), jnp.float32)], axis=1
        )
    tiles = full.shape[1] // LANES
    lane = lax.broadcasted_iota(jnp.int32, (RANK, LANES), 1)

    def lane_window(block, shift):
        if width < LANES:
            rolled = block if shift == 0 else jnp.where(
                lane < width - shift, pltpu.roll(block, LANES - shift, 1),
                pltpu.roll(block, (width - shift) % LANES, 1),
            )
            return rolled
        first, inner = shift // LANES, shift % LANES
        a = block[:, LANES * first : LANES * first + LANES]
        if inner == 0:
            return a
        nxt = (first + 1) % tiles
        bb = block[:, LANES * nxt : LANES * nxt + LANES]
        return jnp.where(
            lane < LANES - inner, pltpu.roll(a, LANES - inner, 1), pltpu.roll(bb, LANES - inner, 1)
        )

    pieces = []
    for b in range(ny):
        window = lane_window(full[RANK * b : RANK * b + RANK], RANK * b)
        pieces.append(jnp.where(lane < RANK * near, window, 0.0))
    extra = jnp.zeros((RANK, LANES), jnp.float32)
    for q in range(near):
        col = RANK * (q + near)
        tile, inner = col // LANES, col % LANES
        block = full[RANK * q : RANK * q + RANK, LANES * tile : LANES * tile + LANES]
        shift = (RANK * q - inner) % LANES
        if shift:
            block = pltpu.roll(block, shift, 1)
        extra = jnp.where((lane >= RANK * q) & (lane < RANK * q + RANK), block, extra)
    pieces.append(extra)
    tall = g2_part.shape[0] * g2_part.shape[1] - RANK * (ny + 1)
    if tall:
        pieces.append(jnp.zeros((tall, LANES), jnp.float32))
    g2_part[...] = jnp.concatenate(pieces, axis=0).reshape(g2_part.shape)
    copies = exchange(nxc, p, dev_xc, lambda q: g2_part.at[q], g2_rs.at[p])
    g2_rs[p] = g2_part[p]
    arrive(copies)
    g2_y[y] = jnp.sum(g2_rs[...], axis=0)
    copies = exchange(ny, y, dev_y, lambda q: g2_y.at[y], g2_y.at[y])
    arrive(copies)
    g2_z[z] = jnp.sum(g2_y[...], axis=0)
    copies = exchange(nz, z, dev_z, lambda q: g2_z.at[z], g2_z.at[z])
    arrive(copies)
    g2_ag[p] = jnp.sum(g2_z[...], axis=0)
    copies = exchange(nxc, p, dev_xc, lambda q: g2_ag.at[p], g2_ag.at[p])
    arrive(copies)
    flat = g2_ag[...].reshape(g2_ag.shape[0] * g2_ag.shape[1], LANES)

    zero = jnp.zeros((RANK, LANES), jnp.float32)
    upper = [[None] * tiles for _ in range(ny)]
    extra = flat[RANK * ny : RANK * ny + RANK]
    for b in range(ny):
        block = flat[RANK * b : RANK * b + RANK]
        block = jnp.where(lane < RANK, 0.5 * block, block)
        for tile in range(tiles):
            got = zero
            for off in range(near):
                col = (RANK * (b + off)) % width
                if col // LANES != tile:
                    continue
                inner = col % LANES
                shift = (inner - RANK * off) % LANES
                moved = pltpu.roll(block, shift, 1) if shift else block
                got = jnp.where((lane >= inner) & (lane < inner + RANK), moved, got)
            if b < near:
                col = RANK * (b + near)
                if col // LANES == tile:
                    inner = col % LANES
                    shift = (inner - RANK * b) % LANES
                    moved = pltpu.roll(extra, shift, 1) if shift else extra
                    got = jnp.where((lane >= inner) & (lane < inner + RANK), moved, got)
            upper[b][tile] = got
    per_tile = LANES // RANK

    def tile_value(i, j):
        rows = [upper[b][j] for b in range(per_tile * i, min(per_tile * i + per_tile, ny))]
        rows += [zero] * (per_tile - len(rows))
        return jnp.concatenate(rows, axis=0)

    up = [[tile_value(i, j) for j in range(tiles)] for i in range(tiles)]
    sym = [[up[i][j] + up[j][i].T for j in range(tiles)] for i in range(tiles)]

    if tiles == 2:
        halves = merge_pairs([sym[0][0], sym[1][1]])
        halves = [rounded(h) for h in halves]
        crossed = matmul_t(matmul(halves[0], sym[0][1]), halves[1])
        zeros64 = jnp.zeros((64, LANES), jnp.float32)

        def spread(a, b):
            return jnp.concatenate([a, b, zeros64], axis=0)

        pad = jnp.zeros((RANK, LANES), jnp.float32)
        first = spread(halves[0], pad)
        second = spread(pad, halves[1])
        upper_part = matmul_t(matmul(first, sym[0][1]), second)
        last = (
            matmul_t(matmul(first, sym[0][0]), first)
            + matmul_t(matmul(second, sym[1][1]), second)
            + upper_part
            + upper_part.T
        )
        sources = [first, second]
    elif ny == 4:
        tops = top_rows([(sym[0][0], 0), (sym[0][0], 1)])
        joined = jnp.concatenate(
            [rounded(tops[0]), rounded(tops[1]), jnp.zeros((64, LANES), jnp.float32)], axis=0
        )
        last = matmul_t(matmul(joined, sym[0][0]), joined)
        sources = [joined]
    else:
        last = sym[0][0]
        row = lax.broadcasted_iota(jnp.int32, (LANES, LANES), 0)
        col = lax.broadcasted_iota(jnp.int32, (LANES, LANES), 1)
        sources = [jnp.where(row == col, 1.0, 0.0).astype(jnp.float32)]
    top = rounded(top_rows([(last, 0)])[0])
    bent = matmul(top, last)
    place = jnp.concatenate(
        [jnp.zeros((64, LANES), jnp.float32), top, jnp.zeros((32, LANES), jnp.float32)], axis=0
    )
    final = factor_rows(top + matmul_t(bent, place), 64)
    final = jnp.where(half_mask(RANK, 0), final, 0.0)
    weights = jnp.concatenate([matmul(final, s) for s in sources], axis=1)[:, :big]
    weights = weights.astype(jnp.bfloat16)

    mine = half * c + per * y
    for r in range(per):
        tall_rows = jnp.concatenate([a_all[b, r] for b in range(ny)], axis=0)
        f_all[mine + r] = dot(weights, tall_rows, ((1,), (0,))).astype(jnp.bfloat16)
    here = f_all.at[pl.ds(mine, per)]
    copies = exchange(ny, y, dev_y, lambda q: here, here)
    stage = stage_count[0]
    stage_count[0] += 1

    def hand_over(d):
        owner = lax.rem(y + ny - d, ny)
        block = f_all.at[pl.ds(half * c + per * owner, per)]
        copy = pltpu.make_async_remote_copy(
            src_ref=block, dst_ref=block,
            send_sem=send.at[stage, d], recv_sem=recv.at[stage, d],
            device_id=partner, device_id_type=MESH,
        )
        copy.start()
        pending.append(copy)
        return copy

    handed = [hand_over(0)]
    for d in sorted(copies, key=lambda d: min(d, ny - d)):
        copies[d].wait_recv()
        handed.append(hand_over(d))
    for copy in handed:
        copy.wait_recv()

    coef = jnp.zeros((RANK, 64), jnp.float32)
    for r in range(0, 2 * half, 2):
        a = jnp.concatenate([f_all[r], f_all[r + 1]], axis=1)
        b = jnp.concatenate([y_ref[r], y_ref[r + 1]], axis=1)
        coef = coef + dot(a, b, ((1,), (1,)))
    coef_x[x] = jnp.concatenate([coef[:16], coef[16:]], axis=1)
    copies = exchange(nx, x, dev_x, lambda q: coef_x.at[x], coef_x.at[x])
    arrive(copies)
    coef_z[z] = jnp.sum(coef_x[...], axis=0)
    copies = exchange(nz, z, dev_z, lambda q: coef_z.at[z], coef_z.at[z])
    arrive(copies)
    packed = jnp.sum(coef_z[...], axis=0)
    solved = jnp.concatenate([packed[:, :64], packed[:, 64:]], axis=0).astype(jnp.bfloat16)

    solved_t = solved.T
    for r in range(0, out_ref.shape[0]):
        out_ref[r] = dot(solved_t, f_all[r], ((1,), (0,))).astype(jnp.bfloat16)
    for copy in pending:
        copy.wait_send()


def merge_call(rows, ny, nx, nz, height):
    nxc = 2 * nx
    half = rows.shape[0] // 2
    per = half // ny
    tall = RANK * (ny + 1)
    piece2 = -(-tall // (8 * nxc)) * 8
    f32, bf16 = jnp.float32, jnp.bfloat16
    vm = pltpu.VMEM
    return pl.pallas_call(
        functools.partial(merge_kernel, ny, nx, nz),
        out_shape=jax.ShapeDtypeStruct((height, 64, LANES), bf16),
        in_specs=[pl.BlockSpec(memory_space=pltpu.VMEM)],
        out_specs=pl.BlockSpec(memory_space=pltpu.VMEM),
        scratch_shapes=[
            vm((2, half, 64, LANES), bf16),
            vm((nxc, LANES // nxc, LANES), f32),
            vm((nxc, LANES // nxc, LANES), f32),
            vm((nz, LANES // nxc, LANES), f32),
            vm((nxc, LANES // nxc, LANES), f32),
            vm((half, RANK, LANES), bf16),
            vm((ny, per, RANK, LANES), bf16),
            vm((nxc, piece2, LANES), f32),
            vm((nxc, piece2, LANES), f32),
            vm((ny, piece2, LANES), f32),
            vm((nz, piece2, LANES), f32),
            vm((nxc, piece2, LANES), f32),
            vm((2 * half, RANK, LANES), bf16),
            vm((nx, 16, LANES), f32),
            vm((nz, 16, LANES), f32),
            pltpu.SemaphoreType.DMA((13, max(8, nxc, ny, nz))),
            pltpu.SemaphoreType.DMA((13, max(8, nxc, ny, nz))),
        ],
        compiler_params=pltpu.CompilerParams(collective_id=0, has_side_effects=True),
        name="merge",
    )(rows)


def with_halo(block, sides, width, periodic):
    for axis, dim in sides:
        count = lax.axis_size(axis)
        forward = [(i, i + 1) for i in range(count - 1)]
        if periodic:
            forward.append((count - 1, 0))
        backward = [(target, source) for source, target in forward]
        low = lax.ppermute(
            lax.slice_in_dim(block, block.shape[dim] - width, None, axis=dim), axis, forward
        )
        high = lax.ppermute(lax.slice_in_dim(block, 0, width, axis=dim), axis, backward)
        block = jnp.concatenate([low, block, high], axis=dim)
    return block


def stencil(current, coeffs):
    center = current[:, 1:-1, 1:-1]
    middle = coeffs[:, 1:-1, 1:-1]
    northward = 0.5 * (middle + coeffs[:, :-2, 1:-1]) * (current[:, :-2, 1:-1] - center)
    southward = 0.5 * (middle + coeffs[:, 2:, 1:-1]) * (current[:, 2:, 1:-1] - center)
    westward = 0.5 * (middle + coeffs[:, 1:-1, :-2]) * (current[:, 1:-1, :-2] - center)
    eastward = 0.5 * (middle + coeffs[:, 1:-1, 2:]) * (current[:, 1:-1, 2:] - center)
    return center + (northward + southward + westward + eastward)


def shards(residuals, diffusivity):
    snap_count, height, width = residuals.shape
    current = residuals.astype(jnp.float32)
    coeffs = diffusivity[None]
    for pass_index in range(PASSES):
        field_ext, coeff_ext = (
            with_halo(current.astype(jnp.bfloat16), (("lon", 2),), 1, True).astype(current.dtype),
            with_halo(coeffs.astype(jnp.bfloat16), (("lon", 2),), 1, True).astype(coeffs.dtype),
        )
        field_ext, coeff_ext = (
            with_halo(field_ext.astype(jnp.bfloat16), (("lat", 1),), 1, False).astype(
                field_ext.dtype
            ),
            with_halo(coeff_ext.astype(jnp.bfloat16), (("lat", 1),), 1, False).astype(
                coeff_ext.dtype
            ),
        )
        current = stencil(field_ext, coeff_ext)
    rows = (lax.axis_index("lat") * height + jnp.arange(height)).astype(jnp.float32)
    latitude = (rows + 0.5) * math.pi / (height * lax.axis_size("lat")) - math.pi / 2
    scale = jnp.sqrt(jnp.cos(latitude))
    weighted = (current * scale[None, :, None]).astype(jnp.bfloat16)

    ny, nx, nz = lax.axis_size("tm") // 2, lax.axis_size("lat"), lax.axis_size("lon")
    unit = 2 * ny
    padded = -(-height // unit) * unit
    while (padded // 2) % 2:
        padded += unit
    rows = jnp.pad(weighted.transpose(1, 0, 2), ((0, padded - height), (0, 0), (0, 0)))
    projected = merge_call(rows, ny, nx, nz, height)
    return projected.transpose(1, 0, 2)


def solution(mesh):
    return jax.shard_map(
        shards,
        mesh=mesh,
        in_specs=(P("tm", "lat", "lon"), P("lat", "lon")),
        out_specs=P("tm", "lat", "lon"),
        check_vma=False,
    )
```

time: 1150 us -> 228 us (0.20)
  the two profiles are of different devices: /device:TPU:24 before, /device:TPU:1 now
where the time goes in v1:
time: 228 us; the launch traced here: 227 us
  Pallas kernels  124 us (54%)
  starting transfers between devices  61.4 us (27%)
  waiting for transfers between devices  17.3 us (8%)
  local copies, waits for them, and re-layouts  12.5 us (5%)
  other arithmetic  11.5 us (5%)
    pallas_call x1, Pallas kernels, merge_call(): pl.pallas_call(functools.partial(merge_kernel, ny, nx, nz), out_shape=jax...  124 us
    ppermute x10, starting transfers between devices, with_halo(): lax.ppermute(lax.slice_in_dim(block, 0, width, axis=dim), axis, backward)  34.2 us
    ppermute x10, starting transfers between devices, with_halo(): lax.ppermute(lax.slice_in_dim(block, block.shape[dim] - width, None, axis...  27.2 us
    ppermute x10, waiting for transfers between devices, with_halo(): lax.ppermute(lax.slice_in_dim(block, 0, width, axis=dim), axis, backward)  14 us
    convert_element_type x3, other arithmetic, shards(): current.astype(jnp.bfloat16)  4.89 us
  transfers between devices with their start and end apart: 20, of which 8 were waited for; matrix products, arithmetic and copies ran while one was open for 2% of the time, Pallas kernels for 0%

profile of v1, /device:TPU:1, one launch (start us, length us, event | category | flops | bytes accessed | tf_op | source)
XLA Modules:
  0.0 227.4 jit_solution(850300481710846994)
XLA Ops:
  0.0 0.7 convert_bitcast_fusion
  0.8 4.8 %collective-permute-start.4 = (bf16[1,45,1]{2,1,0:T(8,128)(2,1)S(1)}, bf16[1,45,1]{2,1,0:T(8,128)(2,1)S(1)}, u32[]{:S(2)}, u32[]{:S(2)}) collective-permute-start(bf16[1,45,1]{2,1,0:T(8,128)(2,1)S(1)} %get-tuple-element.27), channel_id=1, source_target_pairs={{0,1},{1,2},{2,3},{3,4},{4,5},{5,6},{6,7},{7,0},{8,9},{9,10},{10,1... | collective-permute-start | bytes 278 | tf_op jit(solution)/shard_map/ppermute | solution.py:473
  5.6 8.6 %collective-permute-start.5 = (bf16[1,45,1]{2,1,0:T(8,128)(2,1)S(1)}, bf16[1,45,1]{2,1,0:T(8,128)(2,1)S(1)}, u32[]{:S(2)}, u32[]{:S(2)}) collective-permute-start(bf16[1,45,1]{2,1,0:T(8,128)(2,1)S(1)} %get-tuple-element.28), channel_id=1, source_target_pairs={{1,0},{2,1},{3,2},{4,3},{5,4},{6,5},{7,6},{0,7},{9,8},{10,9},{11,1... | collective-permute-start | bytes 278 | tf_op jit(solution)/shard_map/ppermute | solution.py:476
  14.2 1.8 fusion.49
  16.0 0.4 copy.19
  16.5 3.1 %collective-permute-start.6 = (bf16[1,1,130]{2,1,0:T(2,128)(2,1)S(1)}, bf16[1,1,130]{2,1,0:T(2,128)(2,1)S(1)}, u32[]{:S(2)}, u32[]{:S(2)}) collective-permute-start(bf16[1,1,130]{2,1,0:T(2,128)(2,1)S(1)} %get-tuple-element.25), channel_id=1, source_target_pairs={{0,8},{8,16},{16,24},{1,9},{9,17},{17,25},{2,10},{10,18},{18,26},{... | collective-permute-start | bytes 788 | tf_op jit(solution)/shard_map/ppermute | solution.py:473
  19.6 1.3 collective-permute-start.7
  20.9 1.9 collective-permute-start
  22.9 0.4 copy.20
  23.2 4.6 %collective-permute-start.1 = (bf16[64,45,1]{0,1,2:T(8,128)(2,1)S(1)}, bf16[64,45,1]{0,1,2:T(8,128)(2,1)S(1)}, u32[]{:S(2)}, u32[]{:S(2)}) collective-permute-start(bf16[64,45,1]{0,1,2:T(8,128)(2,1)S(1)} %copy.20), channel_id=1, source_target_pairs={{1,0},{2,1},{3,2},{4,3},{5,4},{6,5},{7,6},{0,7},{9,8},{10,9},{11,1... | collective-permute-start | bytes 17288 | tf_op jit(solution)/shard_map/ppermute | solution.py:476
  27.9 0.4 copy.5
  28.6 0.5 copy.6
  29.2 4.0 %collective-permute-start.2 = (bf16[64,1,130]{2,0,1:T(8,128)(2,1)S(1)}, bf16[64,1,130]{2,0,1:T(8,128)(2,1)S(1)}, u32[]{:S(2)}, u32[]{:S(2)}) collective-permute-start(bf16[64,1,130]{2,0,1:T(8,128)(2,1)S(1)} %get-tuple-element.11), channel_id=1, source_target_pairs={{0,8},{8,16},{16,24},{1,9},{9,17},{17,25},{2,10},{10,18},{18,26},{... | collective-permute-start | bytes 49928 | tf_op jit(solution)/shard_map/ppermute | solution.py:473
  33.2 1.3 collective-permute-start.3
  34.6 3.2 %collective-permute-done.3 = bf16[64,1,130]{2,0,1:T(8,128)(2,1)S(1)} collective-permute-done((bf16[64,1,130]{2,0,1:T(8,128)(2,1)S(1)}, bf16[64,1,130]{2,0,1:T(8,128)(2,1)S(1)}, u32[]{:S(2)}, u32[]{:S(2)}) %collective-permute-start.3) | collective-permute-done | bytes 16672 | tf_op jit(solution)/shard_map/ppermute | solution.py:476
  37.8 0.8 maximum_convert_fusion
  38.7 1.6 fusion.31
  41.0 4.8 %collective-permute-start.9 = (bf16[64,45,1]{0,1,2:T(8,128)(2,1)S(1)}, bf16[64,45,1]{0,1,2:T(8,128)(2,1)S(1)}, u32[]{:S(2)}, u32[]{:S(2)}) collective-permute-start(bf16[64,45,1]{0,1,2:T(8,128)(2,1)S(1)} %copy.8), channel_id=1, source_target_pairs={{1,0},{2,1},{3,2},{4,3},{5,4},{6,5},{7,6},{0,7},{9,8},{10,9},{11,1... | collective-permute-start | bytes 17288 | tf_op jit(solution)/shard_map/ppermute | solution.py:476
  46.2 1.9 collective-permute-start.8
  48.2 0.4 copy.10
  48.6 3.3 %collective-permute-done.8 = bf16[64,45,1]{0,1,2:T(8,128)(2,1)S(1)} collective-permute-done((bf16[64,45,1]{0,1,2:T(8,128)(2,1)S(1)}, bf16[64,45,1]{0,1,2:T(8,128)(2,1)S(1)}, u32[]{:S(2)}, u32[]{:S(2)}) %collective-permute-start.8) | collective-permute-done | bytes 5792 | tf_op jit(solution)/shard_map/ppermute | solution.py:473
  51.9 0.5 copy.9
  52.4 3.4 %collective-permute-start.10 = (bf16[64,1,130]{2,0,1:T(8,128)(2,1)S(1)}, bf16[64,1,130]{2,0,1:T(8,128)(2,1)S(1)}, u32[]{:S(2)}, u32[]{:S(2)}) collective-permute-start(bf16[64,1,130]{2,0,1:T(8,128)(2,1)S(1)} %get-tuple-element.9), channel_id=1, source_target_pairs={{0,8},{8,16},{16,24},{1,9},{9,17},{17,25},{2,10},{10,18},{18,26},{... | collective-permute-start | bytes 49928 | tf_op jit(solution)/shard_map/ppermute | solution.py:473
  55.9 1.3 collective-permute-start.11
  57.2 3.3 %collective-permute-done.11 = bf16[64,1,130]{2,0,1:T(8,128)(2,1)S(1)} collective-permute-done((bf16[64,1,130]{2,0,1:T(8,128)(2,1)S(1)}, bf16[64,1,130]{2,0,1:T(8,128)(2,1)S(1)}, u32[]{:S(2)}, u32[]{:S(2)}) %collective-permute-start.11) | collective-permute-done | bytes 16672 | tf_op jit(solution)/shard_map/ppermute | solution.py:476
  60.5 0.8 maximum_convert_fusion.1
  61.4 1.6 fusion.22
  63.7 1.9 collective-permute-start.12
  66.0 4.6 %collective-permute-start.13 = (bf16[64,45,1]{0,1,2:T(8,128)(2,1)S(1)}, bf16[64,45,1]{0,1,2:T(8,128)(2,1)S(1)}, u32[]{:S(2)}, u32[]{:S(2)}) collective-permute-start(bf16[64,45,1]{0,1,2:T(8,128)(2,1)S(1)} %copy.12), channel_id=1, source_target_pairs={{1,0},{2,1},{3,2},{4,3},{5,4},{6,5},{7,6},{0,7},{9,8},{10,9},{11,1... | collective-permute-start | bytes 17288 | tf_op jit(solution)/shard_map/ppermute | solution.py:476
  70.6 0.4 copy.13
  71.4 0.5 copy.14
  72.0 2.5 %collective-permute-start.14 = (bf16[64,1,130]{2,0,1:T(8,128)(2,1)S(1)}, bf16[64,1,130]{2,0,1:T(8,128)(2,1)S(1)}, u32[]{:S(2)}, u32[]{:S(2)}) collective-permute-start(bf16[64,1,130]{2,0,1:T(8,128)(2,1)S(1)} %get-tuple-element.7), channel_id=1, source_target_pairs={{0,8},{8,16},{16,24},{1,9},{9,17},{17,25},{2,10},{10,18},{18,26},{... | collective-permute-start | bytes 49928 | tf_op jit(solution)/shard_map/ppermute | solution.py:473
  74.5 1.5 collective-permute-start.15
  76.0 3.2 %collective-permute-done.15 = bf16[64,1,130]{2,0,1:T(8,128)(2,1)S(1)} collective-permute-done((bf16[64,1,130]{2,0,1:T(8,128)(2,1)S(1)}, bf16[64,1,130]{2,0,1:T(8,128)(2,1)S(1)}, u32[]{:S(2)}, u32[]{:S(2)}) %collective-permute-start.15) | collective-permute-done | bytes 16672 | tf_op jit(solution)/shard_map/ppermute | solution.py:476
  79.1 0.8 maximum_convert_fusion.2
  80.0 1.6 fusion.13
  82.3 1.9 collective-permute-start.16
  84.6 5.0 %collective-permute-start.17 = (bf16[64,45,1]{0,1,2:T(8,128)(2,1)S(1)}, bf16[64,45,1]{0,1,2:T(8,128)(2,1)S(1)}, u32[]{:S(2)}, u32[]{:S(2)}) collective-permute-start(bf16[64,45,1]{0,1,2:T(8,128)(2,1)S(1)} %copy.16), channel_id=1, source_target_pairs={{1,0},{2,1},{3,2},{4,3},{5,4},{6,5},{7,6},{0,7},{9,8},{10,9},{11,1... | collective-permute-start | bytes 17288 | tf_op jit(solution)/shard_map/ppermute | solution.py:476
  89.7 0.4 copy.17
  90.5 0.5 copy.18
  91.0 1.7 collective-permute-start.18
  92.8 1.3 collective-permute-start.19
  94.1 3.3 %collective-permute-done.19 = bf16[64,1,130]{2,0,1:T(8,128)(2,1)S(1)} collective-permute-done((bf16[64,1,130]{2,0,1:T(8,128)(2,1)S(1)}, bf16[64,1,130]{2,0,1:T(8,128)(2,1)S(1)}, u32[]{:S(2)}, u32[]{:S(2)}) %collective-permute-start.19) | collective-permute-done | bytes 16672 | tf_op jit(solution)/shard_map/ppermute | solution.py:476
  97.4 0.8 maximum_convert_fusion.3
  98.2 1.8 fusion.37
  100.1 1.0 pad.4.y_ref
  101.1 124.3 %merge.1 = bf16[45,64,128]{2,1,0:T(8,128)(2,1)} custom-call(bf16[48,64,128]{2,1,0:T(8,128)(2,1)} %pad.4.y_ref), custom_call_target="tpu_custom_call" | custom-call | tf_op jit(solution)/shard_map/merge/pallas_call | solution.py:437
  225.4 2.0 copy.22
  (35 shorter events, 5.0 us)
Async XLA Ops:
  0.8 15.6 %collective-permute-start.4 = (bf16[1,45,1]{2,1,0:T(8,128)(2,1)S(1)}, bf16[1,45,1]{2,1,0:T(8,128)(2,1)S(1)}, u32[]{:S(2)}, u32[]{:S(2)}) collective-permute-start(bf16[1,45,1]{2,1,0:T(8,128)(2,1)S(1)} %get-tuple-element.27), channel_id=1, source_target_pairs={{0,1},{1,2},{2,3},{3,4},{4,5},{5,6},{6,7},{7,0},{8,9},{9,10},{10,1... | collective-permute-start | bytes 278 | tf_op jit(solution)/shard_map/ppermute | solution.py:473
  5.6 10.8 %collective-permute-start.5 = (bf16[1,45,1]{2,1,0:T(8,128)(2,1)S(1)}, bf16[1,45,1]{2,1,0:T(8,128)(2,1)S(1)}, u32[]{:S(2)}, u32[]{:S(2)}) collective-permute-start(bf16[1,45,1]{2,1,0:T(8,128)(2,1)S(1)} %get-tuple-element.28), channel_id=1, source_target_pairs={{1,0},{2,1},{3,2},{4,3},{5,4},{6,5},{7,6},{0,7},{9,8},{10,9},{11,1... | collective-permute-start | bytes 278 | tf_op jit(solution)/shard_map/ppermute | solution.py:476
  16.0 13.0 %copy-start = (bf16[64,45,128]{2,0,1:T(8,128)(2,1)S(1)}, bf16[64,45,128]{2,0,1:T(8,128)(2,1)}, u32[]{:S(2)}) copy-start(bf16[64,45,128]{2,0,1:T(8,128)(2,1)} %param.2) | copy-start | bytes 2211844
  16.5 11.3 %collective-permute-start.6 = (bf16[1,1,130]{2,1,0:T(2,128)(2,1)S(1)}, bf16[1,1,130]{2,1,0:T(2,128)(2,1)S(1)}, u32[]{:S(2)}, u32[]{:S(2)}) collective-permute-start(bf16[1,1,130]{2,1,0:T(2,128)(2,1)S(1)} %get-tuple-element.25), channel_id=1, source_target_pairs={{0,8},{8,16},{16,24},{1,9},{9,17},{17,25},{2,10},{10,18},{18,26},{... | collective-permute-start | bytes 788 | tf_op jit(solution)/shard_map/ppermute | solution.py:473
  19.6 8.2 %collective-permute-start.7 = (bf16[1,1,130]{2,1,0:T(2,128)(2,1)S(1)}, bf16[1,1,130]{2,1,0:T(2,128)(2,1)S(1)}, u32[]{:S(2)}, u32[]{:S(2)}) collective-permute-start(bf16[1,1,130]{2,1,0:T(2,128)(2,1)S(1)} %get-tuple-element.26), channel_id=1, source_target_pairs={{8,0},{16,8},{24,16},{9,1},{17,9},{25,17},{10,2},{18,10},{26,18},{... | collective-permute-start | bytes 788 | tf_op jit(solution)/shard_map/ppermute | solution.py:476
  20.9 7.0 %collective-permute-start = (bf16[64,45,1]{0,1,2:T(8,128)(2,1)S(1)}, bf16[64,45,1]{0,1,2:T(8,128)(2,1)S(1)}, u32[]{:S(2)}, u32[]{:S(2)}) collective-permute-start(bf16[64,45,1]{0,1,2:T(8,128)(2,1)S(1)} %copy.19), channel_id=1, source_target_pairs={{0,1},{1,2},{2,3},{3,4},{4,5},{5,6},{6,7},{7,0},{8,9},{9,10},{10,1... | collective-permute-start | bytes 17288 | tf_op jit(solution)/shard_map/ppermute | solution.py:473
  23.2 5.4 %collective-permute-start.1 = (bf16[64,45,1]{0,1,2:T(8,128)(2,1)S(1)}, bf16[64,45,1]{0,1,2:T(8,128)(2,1)S(1)}, u32[]{:S(2)}, u32[]{:S(2)}) collective-permute-start(bf16[64,45,1]{0,1,2:T(8,128)(2,1)S(1)} %copy.20), channel_id=1, source_target_pairs={{1,0},{2,1},{3,2},{4,3},{5,4},{6,5},{7,6},{0,7},{9,8},{10,9},{11,1... | collective-permute-start | bytes 17288 | tf_op jit(solution)/shard_map/ppermute | solution.py:476
  29.2 5.4 %collective-permute-start.2 = (bf16[64,1,130]{2,0,1:T(8,128)(2,1)S(1)}, bf16[64,1,130]{2,0,1:T(8,128)(2,1)S(1)}, u32[]{:S(2)}, u32[]{:S(2)}) collective-permute-start(bf16[64,1,130]{2,0,1:T(8,128)(2,1)S(1)} %get-tuple-element.11), channel_id=1, source_target_pairs={{0,8},{8,16},{16,24},{1,9},{9,17},{17,25},{2,10},{10,18},{18,26},{... | collective-permute-start | bytes 49928 | tf_op jit(solution)/shard_map/ppermute | solution.py:473
  33.2 4.7 %collective-permute-start.3 = (bf16[64,1,130]{2,0,1:T(8,128)(2,1)S(1)}, bf16[64,1,130]{2,0,1:T(8,128)(2,1)S(1)}, u32[]{:S(2)}, u32[]{:S(2)}) collective-permute-start(bf16[64,1,130]{2,0,1:T(8,128)(2,1)S(1)} %get-tuple-element.12), channel_id=1, source_target_pairs={{8,0},{16,8},{24,16},{9,1},{17,9},{25,17},{10,2},{18,10},{26,18},{... | collective-permute-start | bytes 49928 | tf_op jit(solution)/shard_map/ppermute | solution.py:476
  41.0 7.1 %collective-permute-start.9 = (bf16[64,45,1]{0,1,2:T(8,128)(2,1)S(1)}, bf16[64,45,1]{0,1,2:T(8,128)(2,1)S(1)}, u32[]{:S(2)}, u32[]{:S(2)}) collective-permute-start(bf16[64,45,1]{0,1,2:T(8,128)(2,1)S(1)} %copy.8), channel_id=1, source_target_pairs={{1,0},{2,1},{3,2},{4,3},{5,4},{6,5},{7,6},{0,7},{9,8},{10,9},{11,1... | collective-permute-start | bytes 17288 | tf_op jit(solution)/shard_map/ppermute | solution.py:476
  46.2 5.6 %collective-permute-start.8 = (bf16[64,45,1]{0,1,2:T(8,128)(2,1)S(1)}, bf16[64,45,1]{0,1,2:T(8,128)(2,1)S(1)}, u32[]{:S(2)}, u32[]{:S(2)}) collective-permute-start(bf16[64,45,1]{0,1,2:T(8,128)(2,1)S(1)} %copy.7), channel_id=1, source_target_pairs={{0,1},{1,2},{2,3},{3,4},{4,5},{5,6},{6,7},{7,0},{8,9},{9,10},{10,1... | collective-permute-start | bytes 17288 | tf_op jit(solution)/shard_map/ppermute | solution.py:473
  52.4 4.7 %collective-permute-start.10 = (bf16[64,1,130]{2,0,1:T(8,128)(2,1)S(1)}, bf16[64,1,130]{2,0,1:T(8,128)(2,1)S(1)}, u32[]{:S(2)}, u32[]{:S(2)}) collective-permute-start(bf16[64,1,130]{2,0,1:T(8,128)(2,1)S(1)} %get-tuple-element.9), channel_id=1, source_target_pairs={{0,8},{8,16},{16,24},{1,9},{9,17},{17,25},{2,10},{10,18},{18,26},{... | collective-permute-start | bytes 49928 | tf_op jit(solution)/shard_map/ppermute | solution.py:473
  55.9 4.7 %collective-permute-start.11 = (bf16[64,1,130]{2,0,1:T(8,128)(2,1)S(1)}, bf16[64,1,130]{2,0,1:T(8,128)(2,1)S(1)}, u32[]{:S(2)}, u32[]{:S(2)}) collective-permute-start(bf16[64,1,130]{2,0,1:T(8,128)(2,1)S(1)} %get-tuple-element.10), channel_id=1, source_target_pairs={{8,0},{16,8},{24,16},{9,1},{17,9},{25,17},{10,2},{18,10},{26,18},{... | collective-permute-start | bytes 49928 | tf_op jit(solution)/shard_map/ppermute | solution.py:476
  63.7 6.9 %collective-permute-start.12 = (bf16[64,45,1]{0,1,2:T(8,128)(2,1)S(1)}, bf16[64,45,1]{0,1,2:T(8,128)(2,1)S(1)}, u32[]{:S(2)}, u32[]{:S(2)}) collective-permute-start(bf16[64,45,1]{0,1,2:T(8,128)(2,1)S(1)} %copy.11), channel_id=1, source_target_pairs={{0,1},{1,2},{2,3},{3,4},{4,5},{5,6},{6,7},{7,0},{8,9},{9,10},{10,1... | collective-permute-start | bytes 17288 | tf_op jit(solution)/shard_map/ppermute | solution.py:473
  66.0 5.4 %collective-permute-start.13 = (bf16[64,45,1]{0,1,2:T(8,128)(2,1)S(1)}, bf16[64,45,1]{0,1,2:T(8,128)(2,1)S(1)}, u32[]{:S(2)}, u32[]{:S(2)}) collective-permute-start(bf16[64,45,1]{0,1,2:T(8,128)(2,1)S(1)} %copy.12), channel_id=1, source_target_pairs={{1,0},{2,1},{3,2},{4,3},{5,4},{6,5},{7,6},{0,7},{9,8},{10,9},{11,1... | collective-permute-start | bytes 17288 | tf_op jit(solution)/shard_map/ppermute | solution.py:476
  72.0 4.0 %collective-permute-start.14 = (bf16[64,1,130]{2,0,1:T(8,128)(2,1)S(1)}, bf16[64,1,130]{2,0,1:T(8,128)(2,1)S(1)}, u32[]{:S(2)}, u32[]{:S(2)}) collective-permute-start(bf16[64,1,130]{2,0,1:T(8,128)(2,1)S(1)} %get-tuple-element.7), channel_id=1, source_target_pairs={{0,8},{8,16},{16,24},{1,9},{9,17},{17,25},{2,10},{10,18},{18,26},{... | collective-permute-start | bytes 49928 | tf_op jit(solution)/shard_map/ppermute | solution.py:473
  74.5 4.7 %collective-permute-start.15 = (bf16[64,1,130]{2,0,1:T(8,128)(2,1)S(1)}, bf16[64,1,130]{2,0,1:T(8,128)(2,1)S(1)}, u32[]{:S(2)}, u32[]{:S(2)}) collective-permute-start(bf16[64,1,130]{2,0,1:T(8,128)(2,1)S(1)} %get-tuple-element.8), channel_id=1, source_target_pairs={{8,0},{16,8},{24,16},{9,1},{17,9},{25,17},{10,2},{18,10},{26,18},{... | collective-permute-start | bytes 49928 | tf_op jit(solution)/shard_map/ppermute | solution.py:476
  82.3 7.3 %collective-permute-start.16 = (bf16[64,45,1]{0,1,2:T(8,128)(2,1)S(1)}, bf16[64,45,1]{0,1,2:T(8,128)(2,1)S(1)}, u32[]{:S(2)}, u32[]{:S(2)}) collective-permute-start(bf16[64,45,1]{0,1,2:T(8,128)(2,1)S(1)} %copy.15), channel_id=1, source_target_pairs={{0,1},{1,2},{2,3},{3,4},{4,5},{5,6},{6,7},{7,0},{8,9},{9,10},{10,1... | collective-permute-start | bytes 17288 | tf_op jit(solution)/shard_map/ppermute | solution.py:473
  84.6 5.8 %collective-permute-start.17 = (bf16[64,45,1]{0,1,2:T(8,128)(2,1)S(1)}, bf16[64,45,1]{0,1,2:T(8,128)(2,1)S(1)}, u32[]{:S(2)}, u32[]{:S(2)}) collective-permute-start(bf16[64,45,1]{0,1,2:T(8,128)(2,1)S(1)} %copy.16), channel_id=1, source_target_pairs={{1,0},{2,1},{3,2},{4,3},{5,4},{6,5},{7,6},{0,7},{9,8},{10,9},{11,1... | collective-permute-start | bytes 17288 | tf_op jit(solution)/shard_map/ppermute | solution.py:476
  91.0 3.1 %collective-permute-start.18 = (bf16[64,1,130]{2,0,1:T(8,128)(2,1)S(1)}, bf16[64,1,130]{2,0,1:T(8,128)(2,1)S(1)}, u32[]{:S(2)}, u32[]{:S(2)}) collective-permute-start(bf16[64,1,130]{2,0,1:T(8,128)(2,1)S(1)} %get-tuple-element.5), channel_id=1, source_target_pairs={{0,8},{8,16},{16,24},{1,9},{9,17},{17,25},{2,10},{10,18},{18,26},{... | collective-permute-start | bytes 49928 | tf_op jit(solution)/shard_map/ppermute | solution.py:473
  92.8 4.7 %collective-permute-start.19 = (bf16[64,1,130]{2,0,1:T(8,128)(2,1)S(1)}, bf16[64,1,130]{2,0,1:T(8,128)(2,1)S(1)}, u32[]{:S(2)}, u32[]{:S(2)}) collective-permute-start(bf16[64,1,130]{2,0,1:T(8,128)(2,1)S(1)} %get-tuple-element.6), channel_id=1, source_target_pairs={{8,0},{16,8},{24,16},{9,1},{17,9},{25,17},{10,2},{18,10},{26,18},{... | collective-permute-start | bytes 49928 | tf_op jit(solution)/shard_map/ppermute | solution.py:476

commit v2 on v1

--- a/solution.py
+++ b/solution.py
@@ -12,6 +12,7 @@
 PASSES = 4
 POWER = 3
 LANES = 128
+ROW_BASE = 11
 HIGHEST = lax.Precision.HIGHEST
 MESH = pl.DeviceIdType.MESH
 
@@ -133,11 +134,13 @@
 
 
 def merge_kernel(
-    ny, nx, nz, y_ref, out_ref,
+    ny, nx, nz, res_hbm, dif_ref, out_ref,
+    res_ref, field, west, east, coef_m, coef_s, grid, y_ref, pack, pack_edge, edge_rows, dif_edge,
+    got_rows, got_pack, got_edge, got_dif, got_dif_edge,
     pair, gram_part, gram_rs, gram_z, gram_ag,
     a_own, a_all, g2_part, g2_rs, g2_y, g2_z, g2_ag,
     f_all, coef_x, coef_z,
-    send, recv,
+    send, recv, load_sem,
 ):
     t, x, z = lax.axis_index("tm"), lax.axis_index("lat"), lax.axis_index("lon")
     y, c = t // 2, lax.rem(t, 2)
@@ -159,6 +162,12 @@
         return (q * 2 + c, x, z)
 
     partner = (y * 2 + (1 - c), x, z)
+    def dev_around(dx, dz):
+        return (t, lax.rem(x + dx + nx, nx), lax.rem(z + dz + nz, nz))
+
+    load = pltpu.make_async_copy(res_hbm, res_ref, load_sem)
+    load.start()
+    corners = [(dx, dz) for dx in (-1, 1) for dz in (-1, 1)]
     barrier = pltpu.get_barrier_semaphore()
     groups = ((nxc, p, dev_xc), (nz, z, dev_z), (ny, y, dev_y))
     for n, me, dev in groups:
@@ -166,7 +175,8 @@
             pl.semaphore_signal(
                 barrier, inc=1, device_id=dev(lax.rem(me + d, n)), device_id_type=MESH
             )
-    pl.semaphore_wait(barrier, sum(n - 1 for n, _, _ in groups))
+    for dx, dz in corners:
+        pl.semaphore_signal(barrier, inc=1, device_id=dev_around(dx, dz), device_id_type=MESH)
 
     pending = []
     stage_count = [0]
@@ -190,6 +200,213 @@
     def arrive(copies):
         for d in sorted(copies, key=lambda d: min(d, len(copies) + 1 - d)):
             copies[d].wait_recv()
+
+    height = res_ref.shape[1]
+    base, edge = ROW_BASE, PASSES
+    lane8 = lax.broadcasted_iota(jnp.int32, (8, LANES), 1)
+    lane_h = lax.broadcasted_iota(jnp.int32, (height, LANES), 1)
+    load.wait()
+
+    def take_in(g, carry):
+        def one(j, acc):
+            s = 16 * g + j
+            value = pltpu.roll(res_ref[s].astype(jnp.float32), 8 * j + 4, 1)
+            field[0, s, pl.ds(base, height), :] = value
+            return jnp.where(lane_h // 8 == j, value, acc)
+
+        acc = lax.fori_loop(0, 16, one, jnp.zeros((height, LANES), jnp.float32), unroll=2)
+        west[0, g, pl.ds(base, height), :] = acc
+        east[0, g, pl.ds(base, height), :] = acc
+        pack[g, pl.ds(0, height), :] = acc.astype(jnp.bfloat16)
+        pack_edge[0, g, pl.ds(0, edge), :] = acc[:edge].astype(jnp.bfloat16)
+        pack_edge[1, g, pl.ds(0, edge), :] = acc[height - edge :].astype(jnp.bfloat16)
+        return carry
+
+    lax.fori_loop(0, 4, take_in, 0)
+    for side, first in ((0, 0), (1, height - edge)):
+        for e in range(edge):
+            edge_rows[side, e] = field[0, :, base + first + e, :].astype(jnp.bfloat16)
+    dif_edge[0, pl.ds(0, edge), :] = dif_ref[pl.ds(0, edge), :]
+    dif_edge[1, pl.ds(0, edge), :] = dif_ref[pl.ds(height - edge, edge), :]
+    pl.semaphore_wait(barrier, sum(n - 1 for n, _, _ in groups) + len(corners))
+
+    stage = stage_count[0]
+    stage_count[0] += 3
+    halo = []
+
+    def pass_on(source, target, dx, dz):
+        at = len(halo)
+        copy = pltpu.make_async_remote_copy(
+            src_ref=source, dst_ref=target,
+            send_sem=send.at[stage + at // 8, at % 8], recv_sem=recv.at[stage + at // 8, at % 8],
+            device_id=dev_around(dx, dz), device_id_type=MESH,
+        )
+        copy.start()
+        halo.append(copy)
+        pending.append(copy)
+
+    for side, dx in ((0, -1), (1, 1)):
+        for dz in (-1, 1):
+            pass_on(pack_edge.at[side], got_edge.at[side, dz + 1], dx, dz)
+            pass_on(dif_edge.at[side], got_dif_edge.at[side, dz + 1], dx, dz)
+        pass_on(pack_edge.at[side], got_edge.at[side, 1], dx, 0)
+        pass_on(dif_edge.at[side], got_dif_edge.at[side, 1], dx, 0)
+        pass_on(edge_rows.at[side], got_rows.at[side], dx, 0)
+    for dz in (-1, 1):
+        pass_on(pack, got_pack.at[(dz + 1) // 2], 0, dz)
+        pass_on(dif_ref, got_dif.at[(dz + 1) // 2], 0, dz)
+    for copy in halo:
+        copy.wait_recv()
+
+    has_north, has_south = x > 0, x < nx - 1
+    for side, first, there in ((1, base - edge, has_north), (0, base + height, has_south)):
+        for e in range(edge):
+            row = got_rows[side, e].astype(jnp.float32)
+            row = jnp.where(there, row, 0.0)
+            field[0, :, first + e, :] = row
+
+    def seam(own, other, rows, own_first):
+        t8 = lax.broadcasted_iota(jnp.int32, (rows, LANES), 1) % 8
+        return jnp.where((t8 < 4) == own_first, own, other)
+
+    for g in range(4):
+        own = west[0, g, pl.ds(base, height), :]
+        from_west = got_pack[1, g, pl.ds(0, height), :].astype(jnp.float32)
+        from_east = got_pack[0, g, pl.ds(0, height), :].astype(jnp.float32)
+        west[0, g, pl.ds(base, height), :] = seam(own, from_west, height, False)
+        east[0, g, pl.ds(base, height), :] = seam(own, from_east, height, True)
+        for side, first, there in ((1, base - edge, has_north), (0, base + height, has_south)):
+            own, from_west, from_east = (
+                jnp.where(
+                    there, got_edge[side, k, g, pl.ds(0, edge), :].astype(jnp.float32), 0.0
+                )
+                for k in (1, 2, 0)
+            )
+            west[0, g, pl.ds(first, edge), :] = seam(own, from_west, edge, False)
+            east[0, g, pl.ds(first, edge), :] = seam(own, from_east, edge, True)
+
+    wide = height + 2 * edge
+
+    def tall_of(middle, k):
+        north = jnp.where(has_north, got_dif_edge[1, k, pl.ds(0, edge), :], 0.0)
+        south = jnp.where(has_south, got_dif_edge[0, k, pl.ds(0, edge), :], 0.0)
+        return jnp.concatenate([north, middle, south], axis=0)
+
+    own_d = tall_of(dif_ref[...], 1)
+    west_d = tall_of(got_dif[1], 2)
+    east_d = tall_of(got_dif[0], 0)
+    lane_w = lax.broadcasted_iota(jnp.int32, (wide, LANES), 1)
+    row_w = lax.broadcasted_iota(jnp.int32, (wide, LANES), 0)
+    inside = ((row_w >= edge) | has_north) & ((row_w < height + edge) | has_south)
+
+    def five(center, left, right):
+        zero_row = jnp.zeros((1, LANES), jnp.float32)
+        up = jnp.concatenate([zero_row, center[:-1]], axis=0)
+        down = jnp.concatenate([center[1:], zero_row], axis=0)
+        ks = [jnp.where(inside, 0.5 * (center + v), 0.0) for v in (up, down, left, right)]
+        return [1.0 - (ks[0] + ks[1] + ks[2] + ks[3])] + ks
+
+    left = jnp.where(lane_w == 0, pltpu.roll(west_d, 1, 1), pltpu.roll(own_d, 1, 1))
+    right = jnp.where(lane_w == LANES - 1, pltpu.roll(east_d, LANES - 1, 1), pltpu.roll(own_d, LANES - 1, 1))
+    main = five(own_d, left, right)
+    for k in range(5):
+        coef_m[0, k, pl.ds(base - edge, wide), :] = main[k]
+
+    def turn(j, carry):
+        for k in range(5):
+            coef_m[j, k, pl.ds(base - edge, wide), :] = pltpu.roll(
+                coef_m[0, k, pl.ds(base - edge, wide), :], 8 * j + 4, 1
+            )
+        return carry
+
+    lax.fori_loop(1, 16, turn, 0)
+    for k in range(5):
+        coef_m[0, k, pl.ds(base - edge, wide), :] = pltpu.roll(main[k], 4, 1)
+    for which, (first_d, second_d) in enumerate(((west_d, own_d), (own_d, east_d))):
+        strip = jnp.where(
+            lane_w < 4,
+            pltpu.roll(first_d, 4, 1),
+            jnp.where(lane_w < 8, pltpu.roll(second_d, 4, 1), 0.0),
+        )
+        for shift in (8, 16, 32, 64):
+            strip = strip + pltpu.roll(strip, shift, 1)
+        ks = five(strip, pltpu.roll(strip, 1, 1), pltpu.roll(strip, LANES - 1, 1))
+        for k in range(5):
+            coef_s[which, k, pl.ds(base - edge, wide), :] = ks[k]
+
+    def weighted_sum(c, center, north, south, left, right):
+        return center * c[0] + north * c[1] + south * c[2] + left * c[3] + right * c[4]
+
+    tile_rows = [8 * k for k in range(1, (base + height + edge + 7) // 8)]
+
+    def stencil_rows(src, dst, j, tiles, finish):
+        for r in tiles:
+            here = pl.ds(r, 8)
+            c = [coef_m[j, k, here, :] for k in range(5)]
+            for g in range(4):
+                s = 16 * g + j
+                center = field[src, s, here, :]
+                lft = jnp.where(lane8 == 8 * j + 3, west[src, g, here, :], center)
+                rgt = jnp.where(lane8 == 8 * j + 4, east[src, g, here, :], center)
+                finish(
+                    s, r,
+                    weighted_sum(
+                        c, center, field[src, s, pl.ds(r - 1, 8), :],
+                        field[src, s, pl.ds(r + 1, 8), :],
+                        pltpu.roll(lft, 1, 1), pltpu.roll(rgt, LANES - 1, 1),
+                    ),
+                )
+
+    def one_pass(number, carry):
+        src = lax.rem(number, 2)
+        dst = 1 - src
+
+        def keep(s, r, value):
+            field[dst, s, pl.ds(r, 8), :] = value
+
+        def each(j, inner):
+            stencil_rows(src, dst, j, tile_rows, keep)
+            return inner
+
+        lax.fori_loop(0, 16, each, 0)
+        for which, strip in enumerate((west, east)):
+            for r in tile_rows:
+                here = pl.ds(r, 8)
+                c = [coef_s[which, k, here, :] for k in range(5)]
+                for g in range(4):
+                    center = strip[src, g, here, :]
+                    strip[dst, g, here, :] = weighted_sum(
+                        c, center, strip[src, g, pl.ds(r - 1, 8), :],
+                        strip[src, g, pl.ds(r + 1, 8), :],
+                        pltpu.roll(center, 1, 1), pltpu.roll(center, LANES - 1, 1),
+                    )
+        return carry
+
+    lax.fori_loop(0, PASSES - 1, one_pass, 0)
+    last_rows = [8 * k for k in range(1, (base + height + 7) // 8)]
+    skip = base - 8
+    sub8 = lax.broadcasted_iota(jnp.int32, (8, LANES), 0)
+
+    def scale_of(r):
+        row = (x * height + sub8 + (r - base)).astype(jnp.float32)
+        latitude = (row + 0.5) * math.pi / (height * nx) - math.pi / 2
+        return jnp.sqrt(jnp.maximum(jnp.cos(latitude), 0.0))
+
+    scales = {r: scale_of(r) for r in last_rows}
+
+    def last_pass(j, carry):
+        def out(s, r, value):
+            value = pltpu.roll(value * scales[r], LANES - 4 - 8 * j, 1)
+            grid[pl.ds((r - 8) * 64 + s, 8, stride=64), :] = value
+
+        stencil_rows((PASSES - 1) % 2, None, j, last_rows, out)
+        return carry
+
+    lax.fori_loop(0, 16, last_pass, 0)
+    for i in range(height):
+        y_ref[i] = grid[pl.ds((i + skip) * 64, 64), :].astype(jnp.bfloat16)
+    for i in range(height, y_ref.shape[0]):
+        y_ref[i] = jnp.zeros((64, LANES), jnp.bfloat16)
 
     stage = stage_count[0]
     stage_count[0] += 1
@@ -420,26 +637,61 @@
     solved = jnp.concatenate([packed[:, :64], packed[:, 64:]], axis=0).astype(jnp.bfloat16)
 
     solved_t = solved.T
-    for r in range(0, out_ref.shape[0]):
-        out_ref[r] = dot(solved_t, f_all[r], ((1,), (0,))).astype(jnp.bfloat16)
+    for r in range(height):
+        grid[pl.ds(r * 64, 64), :] = dot(solved_t, f_all[r], ((1,), (0,)))
+
+    def lay_out(s, carry):
+        parts = [
+            grid[pl.ds(8 * k * 64 + s, 8, stride=64), :] for k in range((height + 7) // 8)
+        ]
+        out_ref[s] = jnp.concatenate(parts, axis=0)[:height].astype(jnp.bfloat16)
+        return carry
+
+    lax.fori_loop(0, 64, lay_out, 0, unroll=4)
     for copy in pending:
         copy.wait_send()
 
 
-def merge_call(rows, ny, nx, nz, height):
+def merge_call(residuals, diffusivity, ny, nx, nz):
+    height = residuals.shape[1]
     nxc = 2 * nx
-    half = rows.shape[0] // 2
+    unit = 2 * ny
+    padded = -(-height // unit) * unit
+    while (padded // 2) % 2:
+        padded += unit
+    half = padded // 2
     per = half // ny
     tall = RANK * (ny + 1)
     piece2 = -(-tall // (8 * nxc)) * 8
     f32, bf16 = jnp.float32, jnp.bfloat16
     vm = pltpu.VMEM
+    reach = -(-(ROW_BASE + height + PASSES) // 8) * 8
+    last = -(-(ROW_BASE + height) // 8) * 8
+    tall_h = -(-height // 16) * 16
+    sems = max(8, nxc, ny, nz)
     return pl.pallas_call(
         functools.partial(merge_kernel, ny, nx, nz),
-        out_shape=jax.ShapeDtypeStruct((height, 64, LANES), bf16),
-        in_specs=[pl.BlockSpec(memory_space=pltpu.VMEM)],
+        out_shape=jax.ShapeDtypeStruct(residuals.shape, bf16),
+        in_specs=[pl.BlockSpec(memory_space=pl.ANY), pl.BlockSpec(memory_space=pltpu.VMEM)],
         out_specs=pl.BlockSpec(memory_space=pltpu.VMEM),
         scratch_shapes=[
+            vm(residuals.shape, bf16),
+            vm((2, 64, reach + 8, LANES), f32),
+            vm((2, 4, reach + 8, LANES), f32),
+            vm((2, 4, reach + 8, LANES), f32),
+            vm((16, 5, reach + 8, LANES), f32),
+            vm((2, 5, reach + 8, LANES), f32),
+            vm((max(last - 8, -(-height // 8) * 8) * 64, LANES), f32),
+            vm((padded, 64, LANES), bf16),
+            vm((4, tall_h, LANES), bf16),
+            vm((2, 4, 8, LANES), bf16),
+            vm((2, PASSES, 64, LANES), bf16),
+            vm((2, 8, LANES), f32),
+            vm((2, PASSES, 64, LANES), bf16),
+            vm((2, 4, tall_h, LANES), bf16),
+            vm((2, 3, 4, 8, LANES), bf16),
+            vm((2, height, LANES), f32),
+            vm((2, 3, 8, LANES), f32),
             vm((2, half, 64, LANES), bf16),
             vm((nxc, LANES // nxc, LANES), f32),
             vm((nxc, LANES // nxc, LANES), f32),
@@ -452,73 +704,23 @@
             vm((ny, piece2, LANES), f32),
             vm((nz, piece2, LANES), f32),
             vm((nxc, piece2, LANES), f32),
-            vm((2 * half, RANK, LANES), bf16),
+            vm((padded, RANK, LANES), bf16),
             vm((nx, 16, LANES), f32),
             vm((nz, 16, LANES), f32),
-            pltpu.SemaphoreType.DMA((13, max(8, nxc, ny, nz))),
-            pltpu.SemaphoreType.DMA((13, max(8, nxc, ny, nz))),
+            pltpu.SemaphoreType.DMA((16, sems)),
+            pltpu.SemaphoreType.DMA((16, sems)),
+            pltpu.SemaphoreType.DMA,
         ],
         compiler_params=pltpu.CompilerParams(collective_id=0, has_side_effects=True),
         name="merge",
-    )(rows)
-
-
-def with_halo(block, sides, width, periodic):
-    for axis, dim in sides:
-        count = lax.axis_size(axis)
-        forward = [(i, i + 1) for i in range(count - 1)]
-        if periodic:
-            forward.append((count - 1, 0))
-        backward = [(target, source) for source, target in forward]
-        low = lax.ppermute(
-            lax.slice_in_dim(block, block.shape[dim] - width, None, axis=dim), axis, forward
-        )
-        high = lax.ppermute(lax.slice_in_dim(block, 0, width, axis=dim), axis, backward)
-        block = jnp.concatenate([low, block, high], axis=dim)
-    return block
-
-
-def stencil(current, coeffs):
-    center = current[:, 1:-1, 1:-1]
-    middle = coeffs[:, 1:-1, 1:-1]
-    northward = 0.5 * (middle + coeffs[:, :-2, 1:-1]) * (current[:, :-2, 1:-1] - center)
-    southward = 0.5 * (middle + coeffs[:, 2:, 1:-1]) * (current[:, 2:, 1:-1] - center)
-    westward = 0.5 * (middle + coeffs[:, 1:-1, :-2]) * (current[:, 1:-1, :-2] - center)
-    eastward = 0.5 * (middle + coeffs[:, 1:-1, 2:]) * (current[:, 1:-1, 2:] - center)
-    return center + (northward + southward + westward + eastward)
+    )(residuals, diffusivity)
 
 
 def shards(residuals, diffusivity):
-    snap_count, height, width = residuals.shape
-    current = residuals.astype(jnp.float32)
-    coeffs = diffusivity[None]
-    for pass_index in range(PASSES):
-        field_ext, coeff_ext = (
-            with_halo(current.astype(jnp.bfloat16), (("lon", 2),), 1, True).astype(current.dtype),
-            with_halo(coeffs.astype(jnp.bfloat16), (("lon", 2),), 1, True).astype(coeffs.dtype),
-        )
-        field_ext, coeff_ext = (
-            with_halo(field_ext.astype(jnp.bfloat16), (("lat", 1),), 1, False).astype(
-                field_ext.dtype
-            ),
-            with_halo(coeff_ext.astype(jnp.bfloat16), (("lat", 1),), 1, False).astype(
-                coeff_ext.dtype
-            ),
-        )
-        current = stencil(field_ext, coeff_ext)
-    rows = (lax.axis_index("lat") * height + jnp.arange(height)).astype(jnp.float32)
-    latitude = (rows + 0.5) * math.pi / (height * lax.axis_size("lat")) - math.pi / 2
-    scale = jnp.sqrt(jnp.cos(latitude))
-    weighted = (current * scale[None, :, None]).astype(jnp.bfloat16)
-
-    ny, nx, nz = lax.axis_size("tm") // 2, lax.axis_size("lat"), lax.axis_size("lon")
-    unit = 2 * ny
-    padded = -(-height // unit) * unit
-    while (padded // 2) % 2:
-        padded += unit
-    rows = jnp.pad(weighted.transpose(1, 0, 2), ((0, padded - height), (0, 0), (0, 0)))
-    projected = merge_call(rows, ny, nx, nz, height)
-    return projected.transpose(1, 0, 2)
+    return merge_call(
+        residuals, diffusivity,
+        lax.axis_size("tm") // 2, lax.axis_size("lat"), lax.axis_size("lon"),
+    )
 
 
 def solution(mesh):

time: 228 us -> 240 us (1.053)
  Pallas kernels: 124 us -> 235 us
  starting transfers between devices: 61.4 us -> 0 us
  waiting for transfers between devices: 17.3 us -> 0 us
  other arithmetic: 11.5 us -> 0 us
  local copies, waits for them, and re-layouts: 12.5 us -> 4.67 us
    pallas_call x1, Pallas kernels: 124 us -> 235 us  [merge_call(): pl.pallas_call(functools.partial(merge_kernel, ny, nx, nz), out_shape=jax...]
    ppermute x20 -> x0, starting transfers between devices: 61.4 us -> none  [the longest x10 34.2 us: with_halo(): lax.ppermute(lax.slice_in_dim(block, 0, width, axis=dim), axis, backward)]
    ppermute x20 -> x0, waiting for transfers between devices: 17.3 us -> none  [the longest x10 14 us: with_halo(): lax.ppermute(lax.slice_in_dim(block, 0, width, axis=dim), axis, backward)]
    convert_element_type x9 -> x0, other arithmetic: 9 us -> none  [the longest x3 4.89 us: shards(): current.astype(jnp.bfloat16)]
    slice x11 -> x0, local copies, waits for them, and re-layouts: 5.12 us -> none  [the longest x8 4.01 us: with_halo(): lax.slice_in_dim(block, block.shape[dim] - width, None, axis=dim)]
    ppermute x8 -> x0, local copies, waits for them, and re-layouts: 3.62 us -> none  [the longest x4 1.81 us: with_halo(): lax.ppermute(lax.slice_in_dim(block, 0, width, axis=dim), axis, backward)]
  transfers between devices with their start and end apart: 20 -> 0, of which waited for: 8 -> 0; matrix products, arithmetic and copies ran while one was open for 2% -> 0% of each run, Pallas kernels for 0% -> 0%
where the time goes in v2:
time: 240 us
  Pallas kernels  235 us (98%)
  local copies, waits for them, and re-layouts  4.67 us (2%)
    pallas_call x1, Pallas kernels, merge_call(): pl.pallas_call(functools.partial(merge_kernel, ny, nx, nz), out_shape=jax...  235 us

profile of v2, /device:TPU:1, one launch (start us, length us, event | category | flops | bytes accessed | tf_op | source)
XLA Modules:
  0.0 239.7 jit_solution(8383329527878452046)
XLA Ops:
  0.0 2.5 %copy.3.res_hbm = bf16[64,45,128]{2,1,0:T(8,128)(2,1)} copy(bf16[64,45,128]{2,0,1:T(8,128)(2,1)} %param.2) | data formatting | bytes 1474560 | tf_op args[0]
  2.5 235.1 %merge.1 = bf16[64,45,128]{2,1,0:T(8,128)(2,1)} custom-call(bf16[64,45,128]{2,1,0:T(8,128)(2,1)} %copy.3.res_hbm, f32[45,128]{1,0:T(8,128)} %dif_ref.1), custom_call_target="tpu_custom_call" | custom-call | tf_op jit(solution)/shard_map/merge/pallas_call | solution.py:672
  237.6 2.2 copy.4

commit v3 on v2

--- a/solution.py
+++ b/solution.py
@@ -135,7 +135,7 @@
 
 def merge_kernel(
     ny, nx, nz, res_hbm, dif_ref, out_ref,
-    res_ref, field, west, east, coef_m, coef_s, grid, y_ref, pack, pack_edge, edge_rows, dif_edge,
+    res_ref, field_a, field_b, west_a, west_b, east_a, east_b, coef_0, coef_m, coef_s, grid, y_ref, pack, pack_edge, edge_rows, dif_edge,
     got_rows, got_pack, got_edge, got_dif, got_dif_edge,
     pair, gram_part, gram_rs, gram_z, gram_ag,
     a_own, a_all, g2_part, g2_rs, g2_y, g2_z, g2_ag,
@@ -201,22 +201,27 @@
         for d in sorted(copies, key=lambda d: min(d, len(copies) + 1 - d)):
             copies[d].wait_recv()
 
-    height = res_ref.shape[1]
+    height = res_ref.shape[0]
     base, edge = ROW_BASE, PASSES
     lane8 = lax.broadcasted_iota(jnp.int32, (8, LANES), 1)
     lane_h = lax.broadcasted_iota(jnp.int32, (height, LANES), 1)
     load.wait()
+    for r in range(height):
+        grid[pl.ds(r * 64, 64), :] = res_ref[r].astype(jnp.float32)
 
     def take_in(g, carry):
         def one(j, acc):
             s = 16 * g + j
-            value = pltpu.roll(res_ref[s].astype(jnp.float32), 8 * j + 4, 1)
-            field[0, s, pl.ds(base, height), :] = value
+            parts = [
+                grid[pl.ds(8 * k * 64 + s, 8, stride=64), :] for k in range((height + 7) // 8)
+            ]
+            value = pltpu.roll(jnp.concatenate(parts, axis=0)[:height], 8 * j + 4, 1)
+            field_a[s, pl.ds(base, height), :] = value
             return jnp.where(lane_h // 8 == j, value, acc)
 
-        acc = lax.fori_loop(0, 16, one, jnp.zeros((height, LANES), jnp.float32), unroll=2)
-        west[0, g, pl.ds(base, height), :] = acc
-        east[0, g, pl.ds(base, height), :] = acc
+        acc = lax.fori_loop(0, 16, one, jnp.zeros((height, LANES), jnp.float32), unroll=4)
+        west_a[g, pl.ds(base, height), :] = acc
+        east_a[g, pl.ds(base, height), :] = acc
         pack[g, pl.ds(0, height), :] = acc.astype(jnp.bfloat16)
         pack_edge[0, g, pl.ds(0, edge), :] = acc[:edge].astype(jnp.bfloat16)
         pack_edge[1, g, pl.ds(0, edge), :] = acc[height - edge :].astype(jnp.bfloat16)
@@ -225,7 +230,7 @@
     lax.fori_loop(0, 4, take_in, 0)
     for side, first in ((0, 0), (1, height - edge)):
         for e in range(edge):
-            edge_rows[side, e] = field[0, :, base + first + e, :].astype(jnp.bfloat16)
+            edge_rows[side, e] = field_a[:, base + first + e, :].astype(jnp.bfloat16)
     dif_edge[0, pl.ds(0, edge), :] = dif_ref[pl.ds(0, edge), :]
     dif_edge[1, pl.ds(0, edge), :] = dif_ref[pl.ds(height - edge, edge), :]
     pl.semaphore_wait(barrier, sum(n - 1 for n, _, _ in groups) + len(corners))
@@ -263,18 +268,18 @@
         for e in range(edge):
             row = got_rows[side, e].astype(jnp.float32)
             row = jnp.where(there, row, 0.0)
-            field[0, :, first + e, :] = row
+            field_a[:, first + e, :] = row
 
     def seam(own, other, rows, own_first):
         t8 = lax.broadcasted_iota(jnp.int32, (rows, LANES), 1) % 8
         return jnp.where((t8 < 4) == own_first, own, other)
 
     for g in range(4):
-        own = west[0, g, pl.ds(base, height), :]
+        own = west_a[g, pl.ds(base, height), :]
         from_west = got_pack[1, g, pl.ds(0, height), :].astype(jnp.float32)
         from_east = got_pack[0, g, pl.ds(0, height), :].astype(jnp.float32)
-        west[0, g, pl.ds(base, height), :] = seam(own, from_west, height, False)
-        east[0, g, pl.ds(base, height), :] = seam(own, from_east, height, True)
+        west_a[g, pl.ds(base, height), :] = seam(own, from_west, height, False)
+        east_a[g, pl.ds(base, height), :] = seam(own, from_east, height, True)
         for side, first, there in ((1, base - edge, has_north), (0, base + height, has_south)):
             own, from_west, from_east = (
                 jnp.where(
@@ -282,8 +287,8 @@
                 )
                 for k in (1, 2, 0)
             )
-            west[0, g, pl.ds(first, edge), :] = seam(own, from_west, edge, False)
-            east[0, g, pl.ds(first, edge), :] = seam(own, from_east, edge, True)
+            west_a[g, pl.ds(first, edge), :] = seam(own, from_west, edge, False)
+            east_a[g, pl.ds(first, edge), :] = seam(own, from_east, edge, True)
 
     wide = height + 2 * edge
 
@@ -310,18 +315,16 @@
     right = jnp.where(lane_w == LANES - 1, pltpu.roll(east_d, LANES - 1, 1), pltpu.roll(own_d, LANES - 1, 1))
     main = five(own_d, left, right)
     for k in range(5):
-        coef_m[0, k, pl.ds(base - edge, wide), :] = main[k]
+        coef_0[k, pl.ds(base - edge, wide), :] = main[k]
 
     def turn(j, carry):
         for k in range(5):
             coef_m[j, k, pl.ds(base - edge, wide), :] = pltpu.roll(
-                coef_m[0, k, pl.ds(base - edge, wide), :], 8 * j + 4, 1
+                coef_0[k, pl.ds(base - edge, wide), :], 8 * j + 4, 1
             )
         return carry
 
-    lax.fori_loop(1, 16, turn, 0)
-    for k in range(5):
-        coef_m[0, k, pl.ds(base - edge, wide), :] = pltpu.roll(main[k], 4, 1)
+    lax.fori_loop(0, 16, turn, 0)
     for which, (first_d, second_d) in enumerate(((west_d, own_d), (own_d, east_d))):
         strip = jnp.where(
             lane_w < 4,
@@ -339,50 +342,47 @@
 
     tile_rows = [8 * k for k in range(1, (base + height + edge + 7) // 8)]
 
-    def stencil_rows(src, dst, j, tiles, finish):
+    def stencil_rows(field, west, east, j, tiles, finish):
         for r in tiles:
             here = pl.ds(r, 8)
             c = [coef_m[j, k, here, :] for k in range(5)]
             for g in range(4):
                 s = 16 * g + j
-                center = field[src, s, here, :]
-                lft = jnp.where(lane8 == 8 * j + 3, west[src, g, here, :], center)
-                rgt = jnp.where(lane8 == 8 * j + 4, east[src, g, here, :], center)
+                center = field[s, here, :]
+                lft = jnp.where(lane8 == 8 * j + 3, west[g, here, :], center)
+                rgt = jnp.where(lane8 == 8 * j + 4, east[g, here, :], center)
                 finish(
                     s, r,
                     weighted_sum(
-                        c, center, field[src, s, pl.ds(r - 1, 8), :],
-                        field[src, s, pl.ds(r + 1, 8), :],
+                        c, center, field[s, pl.ds(r - 1, 8), :],
+                        field[s, pl.ds(r + 1, 8), :],
                         pltpu.roll(lft, 1, 1), pltpu.roll(rgt, LANES - 1, 1),
                     ),
                 )
 
-    def one_pass(number, carry):
-        src = lax.rem(number, 2)
-        dst = 1 - src
-
+    def one_pass(field, west, east, field_to, west_to, east_to):
         def keep(s, r, value):
-            field[dst, s, pl.ds(r, 8), :] = value
-
-        def each(j, inner):
-            stencil_rows(src, dst, j, tile_rows, keep)
-            return inner
+            field_to[s, pl.ds(r, 8), :] = value
+
+        def each(j, carry):
+            stencil_rows(field, west, east, j, tile_rows, keep)
+            return carry
 
         lax.fori_loop(0, 16, each, 0)
-        for which, strip in enumerate((west, east)):
+        for which, (strip, strip_to) in enumerate(((west, west_to), (east, east_to))):
             for r in tile_rows:
                 here = pl.ds(r, 8)
                 c = [coef_s[which, k, here, :] for k in range(5)]
                 for g in range(4):
-                    center = strip[src, g, here, :]
-                    strip[dst, g, here, :] = weighted_sum(
-                        c, center, strip[src, g, pl.ds(r - 1, 8), :],
-                        strip[src, g, pl.ds(r + 1, 8), :],
+                    center = strip[g, here, :]
+                    strip_to[g, here, :] = weighted_sum(
+                        c, center, strip[g, pl.ds(r - 1, 8), :], strip[g, pl.ds(r + 1, 8), :],
                         pltpu.roll(center, 1, 1), pltpu.roll(center, LANES - 1, 1),
                     )
-        return carry
-
-    lax.fori_loop(0, PASSES - 1, one_pass, 0)
+
+    states = ((field_a, west_a, east_a), (field_b, west_b, east_b))
+    for number in range(PASSES - 1):
+        one_pass(*states[number % 2], *states[1 - number % 2])
     last_rows = [8 * k for k in range(1, (base + height + 7) // 8)]
     skip = base - 8
     sub8 = lax.broadcasted_iota(jnp.int32, (8, LANES), 0)
@@ -399,7 +399,7 @@
             value = pltpu.roll(value * scales[r], LANES - 4 - 8 * j, 1)
             grid[pl.ds((r - 8) * 64 + s, 8, stride=64), :] = value
 
-        stencil_rows((PASSES - 1) % 2, None, j, last_rows, out)
+        stencil_rows(*states[(PASSES - 1) % 2], j, last_rows, out)
         return carry
 
     lax.fori_loop(0, 16, last_pass, 0)
@@ -638,22 +638,13 @@
 
     solved_t = solved.T
     for r in range(height):
-        grid[pl.ds(r * 64, 64), :] = dot(solved_t, f_all[r], ((1,), (0,)))
-
-    def lay_out(s, carry):
-        parts = [
-            grid[pl.ds(8 * k * 64 + s, 8, stride=64), :] for k in range((height + 7) // 8)
-        ]
-        out_ref[s] = jnp.concatenate(parts, axis=0)[:height].astype(jnp.bfloat16)
-        return carry
-
-    lax.fori_loop(0, 64, lay_out, 0, unroll=4)
+        out_ref[r] = dot(solved_t, f_all[r], ((1,), (0,))).astype(jnp.bfloat16)
     for copy in pending:
         copy.wait_send()
 
 
 def merge_call(residuals, diffusivity, ny, nx, nz):
-    height = residuals.shape[1]
+    height = residuals.shape[0]
     nxc = 2 * nx
     unit = 2 * ny
     padded = -(-height // unit) * unit
@@ -676,9 +667,13 @@
         out_specs=pl.BlockSpec(memory_space=pltpu.VMEM),
         scratch_shapes=[
             vm(residuals.shape, bf16),
-            vm((2, 64, reach + 8, LANES), f32),
-            vm((2, 4, reach + 8, LANES), f32),
-            vm((2, 4, reach + 8, LANES), f32),
+            vm((64, reach + 8, LANES), f32),
+            vm((64, reach + 8, LANES), f32),
+            vm((4, reach + 8, LANES), f32),
+            vm((4, reach + 8, LANES), f32),
+            vm((4, reach + 8, LANES), f32),
+            vm((4, reach + 8, LANES), f32),
+            vm((5, reach + 8, LANES), f32),
             vm((16, 5, reach + 8, LANES), f32),
             vm((2, 5, reach + 8, LANES), f32),
             vm((max(last - 8, -(-height // 8) * 8) * 64, LANES), f32),
@@ -717,10 +712,11 @@
 
 
 def shards(residuals, diffusivity):
-    return merge_call(
-        residuals, diffusivity,
+    projected = merge_call(
+        residuals.transpose(1, 0, 2), diffusivity,
         lax.axis_size("tm") // 2, lax.axis_size("lat"), lax.axis_size("lon"),
     )
+    return projected.transpose(1, 0, 2)
 
 
 def solution(mesh):

time: 240 us -> 141 us (0.59)
  Pallas kernels: 235 us -> 138 us
  local copies, waits for them, and re-layouts: 4.67 us -> 2.03 us
    pallas_call x1, Pallas kernels: 235 us -> 138 us  [merge_call(): pl.pallas_call(functools.partial(merge_kernel, ny, nx, nz), out_shape=jax...]
where the time goes in v3:
time: 141 us; the launch traced here: 140 us
  Pallas kernels  138 us (98%)
  local copies, waits for them, and re-layouts  2.03 us (1%)
    pallas_call x1, Pallas kernels, merge_call(): pl.pallas_call(functools.partial(merge_kernel, ny, nx, nz), out_shape=jax...  138 us

profile of v3, /device:TPU:1, one launch (start us, length us, event | category | flops | bytes accessed | tf_op | source)
XLA Modules:
  0.0 140.4 jit_solution(18392587081706714121)
XLA Ops:
  0.0 138.4 %merge.1 = bf16[45,64,128]{2,1,0:T(8,128)(2,1)} custom-call(bf16[45,64,128]{2,1,0:T(8,128)(2,1)} %bitcast.3, f32[45,128]{1,0:T(8,128)} %dif_ref.1), custom_call_target="tpu_custom_call" | custom-call | tf_op jit(solution)/shard_map/merge/pallas_call | solution.py:663
  138.4 2.0 %copy.4 = bf16[64,45,128]{2,0,1:T(8,128)(2,1)} copy(bf16[64,45,128]{2,0,1:T(8,128)(2,1)} %bitcast.2) | data formatting | bytes 1474560

commit v4 on v3

--- a/solution.py
+++ b/solution.py
@@ -39,7 +39,7 @@
     count = RANK // 8
     v = [m[8 * i : 8 * i + 8] for i in range(count)]
     sub = lax.broadcasted_iota(jnp.int32, (8, LANES), 0)
-    lane = lax.broadcasted_iota(jnp.int32, (8, LANES), 1)
+    pivots = [None] * count
 
     def column(x, j):
         return jnp.broadcast_to(x[:, start + j : start + j + 1], (8, LANES))
@@ -59,6 +59,10 @@
                 row[j] = row[j] - ratio[j] * row[i]
                 for c in cols:
                     c[j] = c[j] - c[i] * ratio[j]
+            kept = pivots[(k + i) // 8]
+            pivots[(k + i) // 8] = (
+                diag[i, i] if kept is None else jnp.where(sub == (k + i) % 8, diag[i, i], kept)
+            )
         scaled = [row[i] * inverse[i] for i in range(block)]
         for i in range(b, count):
             total = None
@@ -72,13 +76,7 @@
                 total = term if total is None else total + term
             if total is not None:
                 v[i] = v[i] - total
-    out = []
-    for i in range(count):
-        pivot = jnp.sum(
-            jnp.where(lane == sub + (start + 8 * i), v[i], 0.0), axis=1, keepdims=True
-        )
-        out.append(v[i] * lax.rsqrt(pivot))
-    return jnp.concatenate(out, axis=0)
+    return jnp.concatenate([v[i] * lax.rsqrt(pivots[i]) for i in range(count)], axis=0)
 
 
 def half_mask(rows, side):
@@ -97,23 +95,20 @@
 
 
 def top_rows(problems):
-    row = lax.broadcasted_iota(jnp.int32, (RANK, LANES), 0)
-    lane = lax.broadcasted_iota(jnp.int32, (RANK, LANES), 1)
-    starts = tuple(
-        jnp.where(lane == row + 64 * side, 1.0, 0.0).astype(jnp.float32) for _, side in problems
-    )
+    def orthonormal(bases):
+        keeps = [half_mask(RANK, side) for _, side in problems]
+        bases = [jnp.where(keep, p, 0.0) for keep, p in zip(keeps, bases)]
+        beside = [inner_beside(p, side) for (_, side), p in zip(problems, bases)]
+        return tuple(
+            jnp.where(keep, factor_rows(m, 64 * (1 - side)), 0.0)
+            for keep, m, (_, side) in zip(keeps, beside, problems)
+        )
 
     def body(_, bases):
-        out = []
-        for (gram, side), p in zip(problems, bases):
-            keep = half_mask(RANK, side)
-            p = jnp.where(keep, matmul(p, gram), 0.0)
-            out.append((inner_beside(p, side), side, keep))
-        return tuple(
-            jnp.where(keep, factor_rows(m, 64 * (1 - side)), 0.0) for m, side, keep in out
-        )
-
-    return lax.fori_loop(0, POWER + 1, body, starts)
+        return orthonormal([matmul(p, gram) for (gram, _), p in zip(problems, bases)])
+
+    start = orthonormal([gram[64 * side : 64 * side + RANK] for gram, side in problems])
+    return lax.fori_loop(0, POWER, body, start)
 
 
 def merge_pairs(grams):
@@ -139,7 +134,7 @@
     got_rows, got_pack, got_edge, got_dif, got_dif_edge,
     pair, gram_part, gram_rs, gram_z, gram_ag,
     a_own, a_all, g2_part, g2_rs, g2_y, g2_z, g2_ag,
-    f_all, coef_x, coef_z,
+    f_all, coef_x, coef_z, top_own, half_own,
     send, recv, load_sem,
 ):
     t, x, z = lax.axis_index("tm"), lax.axis_index("lat"), lax.axis_index("lon")
@@ -207,19 +202,19 @@
     lane_h = lax.broadcasted_iota(jnp.int32, (height, LANES), 1)
     load.wait()
     for r in range(height):
-        grid[pl.ds(r * 64, 64), :] = res_ref[r].astype(jnp.float32)
+        grid[pl.ds(r * 72, 64), :] = res_ref[r].astype(jnp.float32)
 
     def take_in(g, carry):
         def one(j, acc):
             s = 16 * g + j
             parts = [
-                grid[pl.ds(8 * k * 64 + s, 8, stride=64), :] for k in range((height + 7) // 8)
+                grid[pl.ds(8 * k * 72 + s, 8, stride=72), :] for k in range((height + 7) // 8)
             ]
             value = pltpu.roll(jnp.concatenate(parts, axis=0)[:height], 8 * j + 4, 1)
             field_a[s, pl.ds(base, height), :] = value
             return jnp.where(lane_h // 8 == j, value, acc)
 
-        acc = lax.fori_loop(0, 16, one, jnp.zeros((height, LANES), jnp.float32), unroll=4)
+        acc = lax.fori_loop(0, 16, one, jnp.zeros((height, LANES), jnp.float32), unroll=8)
         west_a[g, pl.ds(base, height), :] = acc
         east_a[g, pl.ds(base, height), :] = acc
         pack[g, pl.ds(0, height), :] = acc.astype(jnp.bfloat16)
@@ -324,7 +319,7 @@
             )
         return carry
 
-    lax.fori_loop(0, 16, turn, 0)
+    lax.fori_loop(0, 16, turn, 0, unroll=2)
     for which, (first_d, second_d) in enumerate(((west_d, own_d), (own_d, east_d))):
         strip = jnp.where(
             lane_w < 4,
@@ -368,7 +363,7 @@
             stencil_rows(field, west, east, j, tile_rows, keep)
             return carry
 
-        lax.fori_loop(0, 16, each, 0)
+        lax.fori_loop(0, 16, each, 0, unroll=2)
         for which, (strip, strip_to) in enumerate(((west, west_to), (east, east_to))):
             for r in tile_rows:
                 here = pl.ds(r, 8)
@@ -397,16 +392,28 @@
     def last_pass(j, carry):
         def out(s, r, value):
             value = pltpu.roll(value * scales[r], LANES - 4 - 8 * j, 1)
-            grid[pl.ds((r - 8) * 64 + s, 8, stride=64), :] = value
+            grid[pl.ds((r - 8) * 72 + s, 8, stride=72), :] = value
 
         stencil_rows(*states[(PASSES - 1) % 2], j, last_rows, out)
         return carry
 
-    lax.fori_loop(0, 16, last_pass, 0)
+    lax.fori_loop(0, 16, last_pass, 0, unroll=2)
     for i in range(height):
-        y_ref[i] = grid[pl.ds((i + skip) * 64, 64), :].astype(jnp.bfloat16)
+        y_ref[i] = grid[pl.ds((i + skip) * 72, 64), :].astype(jnp.bfloat16)
     for i in range(height, y_ref.shape[0]):
         y_ref[i] = jnp.zeros((64, LANES), jnp.bfloat16)
+
+    def give(block):
+        at = stage_count[0]
+        stage_count[0] += 1
+        copy = pltpu.make_async_remote_copy(
+            src_ref=block, dst_ref=block,
+            send_sem=send.at[at, 0], recv_sem=recv.at[at, 0],
+            device_id=partner, device_id_type=MESH,
+        )
+        copy.start()
+        pending.append(copy)
+        copy.wait_recv()
 
     stage = stage_count[0]
     stage_count[0] += 1
@@ -440,7 +447,13 @@
     arrive(copies)
     gram = gram_ag[...].reshape(LANES, LANES)
 
-    basis = merge_pairs([gram])[0].astype(jnp.bfloat16)
+    own_gram = jnp.where(c == 0, gram[:64], pltpu.roll(gram[64:], 64, 1))
+    zeros64 = jnp.zeros((64, LANES), jnp.float32)
+    top_own[c] = rounded(top_rows([(jnp.concatenate([own_gram, zeros64], axis=0), 0)])[0])
+    give(top_own.at[c])
+    joined = jnp.concatenate([top_own[0], pltpu.roll(top_own[1], 64, 1), zeros64], axis=0)
+    merged = matmul_t(matmul(joined, gram), joined)
+    basis = matmul(rounded(top_rows([(merged, 0)])[0]), joined).astype(jnp.bfloat16)
 
     for r in range(0, half, 2):
         wide = jnp.concatenate([rows_of(r), rows_of(r + 1)], axis=1)
@@ -507,13 +520,34 @@
     copies = exchange(nxc, p, dev_xc, lambda q: g2_part.at[q], g2_rs.at[p])
     g2_rs[p] = g2_part[p]
     arrive(copies)
-    g2_y[y] = jnp.sum(g2_rs[...], axis=0)
-    copies = exchange(ny, y, dev_y, lambda q: g2_y.at[y], g2_y.at[y])
-    arrive(copies)
-    g2_z[z] = jnp.sum(g2_y[...], axis=0)
-    copies = exchange(nz, z, dev_z, lambda q: g2_z.at[z], g2_z.at[z])
-    arrive(copies)
-    g2_ag[p] = jnp.sum(g2_z[...], axis=0)
+    deep = g2_part.shape[1]
+    cut = -(-deep // 16) * 8
+    low, high = pl.ds(0, cut), pl.ds(cut, deep - cut)
+    share = jnp.sum(g2_rs[...], axis=0)
+    g2_y[y, low, :] = share[:cut]
+    if deep > cut:
+        g2_z[z, high, :] = share[cut:]
+    for order in range(2):
+        along_y, along_z = (low, high) if order == 0 else (high, low)
+        rows_y, rows_z = (cut, deep - cut) if order == 0 else (deep - cut, cut)
+        copies_y, copies_z = {}, {}
+        if rows_y:
+            copies_y = exchange(
+                ny, y, dev_y, lambda q: g2_y.at[y, along_y], g2_y.at[y, along_y]
+            )
+        if rows_z:
+            copies_z = exchange(
+                nz, z, dev_z, lambda q: g2_z.at[z, along_z], g2_z.at[z, along_z]
+            )
+        arrive(copies_y)
+        arrive(copies_z)
+        if order == 0:
+            g2_z[z, low, :] = jnp.sum(g2_y[:, low, :], axis=0)
+            if deep > cut:
+                g2_y[y, high, :] = jnp.sum(g2_z[:, high, :], axis=0)
+    g2_ag[p, low, :] = jnp.sum(g2_z[:, low, :], axis=0)
+    if deep > cut:
+        g2_ag[p, high, :] = jnp.sum(g2_y[:, high, :], axis=0)
     copies = exchange(nxc, p, dev_xc, lambda q: g2_ag.at[p], g2_ag.at[p])
     arrive(copies)
     flat = g2_ag[...].reshape(g2_ag.shape[0] * g2_ag.shape[1], LANES)
@@ -553,10 +587,9 @@
     sym = [[up[i][j] + up[j][i].T for j in range(tiles)] for i in range(tiles)]
 
     if tiles == 2:
-        halves = merge_pairs([sym[0][0], sym[1][1]])
-        halves = [rounded(h) for h in halves]
-        crossed = matmul_t(matmul(halves[0], sym[0][1]), halves[1])
-        zeros64 = jnp.zeros((64, LANES), jnp.float32)
+        half_own[c] = rounded(merge_pairs([jnp.where(c == 0, sym[0][0], sym[1][1])])[0])
+        give(half_own.at[c])
+        halves = [half_own[0], half_own[1]]
 
         def spread(a, b):
             return jnp.concatenate([a, b, zeros64], axis=0)
@@ -627,13 +660,13 @@
         a = jnp.concatenate([f_all[r], f_all[r + 1]], axis=1)
         b = jnp.concatenate([y_ref[r], y_ref[r + 1]], axis=1)
         coef = coef + dot(a, b, ((1,), (1,)))
-    coef_x[x] = jnp.concatenate([coef[:16], coef[16:]], axis=1)
+    coef_x[x] = jnp.concatenate([coef[:16], coef[16:]], axis=1).astype(jnp.bfloat16)
     copies = exchange(nx, x, dev_x, lambda q: coef_x.at[x], coef_x.at[x])
     arrive(copies)
-    coef_z[z] = jnp.sum(coef_x[...], axis=0)
+    coef_z[z] = jnp.sum(coef_x[...].astype(jnp.float32), axis=0).astype(jnp.bfloat16)
     copies = exchange(nz, z, dev_z, lambda q: coef_z.at[z], coef_z.at[z])
     arrive(copies)
-    packed = jnp.sum(coef_z[...], axis=0)
+    packed = jnp.sum(coef_z[...].astype(jnp.float32), axis=0)
     solved = jnp.concatenate([packed[:, :64], packed[:, 64:]], axis=0).astype(jnp.bfloat16)
 
     solved_t = solved.T
@@ -676,7 +709,7 @@
             vm((5, reach + 8, LANES), f32),
             vm((16, 5, reach + 8, LANES), f32),
             vm((2, 5, reach + 8, LANES), f32),
-            vm((max(last - 8, -(-height // 8) * 8) * 64, LANES), f32),
+            vm((max(last - 8, -(-height // 8) * 8) * 72, LANES), f32),
             vm((padded, 64, LANES), bf16),
             vm((4, tall_h, LANES), bf16),
             vm((2, 4, 8, LANES), bf16),
@@ -700,10 +733,12 @@
             vm((nz, piece2, LANES), f32),
             vm((nxc, piece2, LANES), f32),
             vm((padded, RANK, LANES), bf16),
-            vm((nx, 16, LANES), f32),
-            vm((nz, 16, LANES), f32),
-            pltpu.SemaphoreType.DMA((16, sems)),
-            pltpu.SemaphoreType.DMA((16, sems)),
+            vm((nx, 16, LANES), bf16),
+            vm((nz, 16, LANES), bf16),
+            vm((2, RANK, LANES), f32),
+            vm((2, RANK, LANES), f32),
+            pltpu.SemaphoreType.DMA((20, sems)),
+            pltpu.SemaphoreType.DMA((20, sems)),
             pltpu.SemaphoreType.DMA,
         ],
         compiler_params=pltpu.CompilerParams(collective_id=0, has_side_effects=True),

time: 141 us -> 124 us (0.88)
  Pallas kernels: 138 us -> 122 us
    pallas_call x1, Pallas kernels: 138 us -> 122 us  [merge_call(): pl.pallas_call(functools.partial(merge_kernel, ny, nx, nz), out_shape=jax...]
where the time goes in v4:
time: 124 us
  Pallas kernels  122 us (98%)
  local copies, waits for them, and re-layouts  2.03 us (2%)
    pallas_call x1, Pallas kernels, merge_call(): pl.pallas_call(functools.partial(merge_kernel, ny, nx, nz), out_shape=jax...  122 us

profile of v4, /device:TPU:1, one launch (start us, length us, event | category | flops | bytes accessed | tf_op | source)
XLA Modules:
  0.0 124.2 jit_solution(3684831035721230448)
XLA Ops:
  0.0 122.2 %merge.1 = bf16[45,64,128]{2,1,0:T(8,128)(2,1)} custom-call(bf16[45,64,128]{2,1,0:T(8,128)(2,1)} %bitcast.3, f32[45,128]{1,0:T(8,128)} %dif_ref.1), custom_call_target="tpu_custom_call" | custom-call | tf_op jit(solution)/shard_map/merge/pallas_call | solution.py:696
  122.2 2.0 %copy.4 = bf16[64,45,128]{2,0,1:T(8,128)(2,1)} copy(bf16[64,45,128]{2,0,1:T(8,128)(2,1)} %bitcast.2) | data formatting | bytes 1474560

commit v5 on v4

--- a/solution.py
+++ b/solution.py
@@ -129,11 +129,11 @@
 
 
 def merge_kernel(
-    ny, nx, nz, res_hbm, dif_ref, out_ref,
+    ny, nx, nz, res_hbm, dif_ref, solved_out, f_out,
     res_ref, field_a, field_b, west_a, west_b, east_a, east_b, coef_0, coef_m, coef_s, grid, y_ref, pack, pack_edge, edge_rows, dif_edge,
     got_rows, got_pack, got_edge, got_dif, got_dif_edge,
-    pair, gram_part, gram_rs, gram_z, gram_ag,
-    a_own, a_all, g2_part, g2_rs, g2_y, g2_z, g2_ag,
+    pair, y_all, basis_all, own_blocks, gram_part, gram_rs, gram_z, gram_ag,
+    a_all, g2_part, g2_rs, g2_y, g2_z, g2_ag,
     f_all, coef_x, coef_z, top_own, half_own,
     send, recv, load_sem,
 ):
@@ -418,17 +418,20 @@
     stage = stage_count[0]
     stage_count[0] += 1
     swap = pltpu.make_async_remote_copy(
-        src_ref=y_ref.at[pl.ds(half * (1 - c), half)], dst_ref=pair.at[c],
+        src_ref=y_ref.at[pl.ds(half * (1 - c), half)], dst_ref=pair.at[:, c],
         send_sem=send.at[stage, 0], recv_sem=recv.at[stage, 0],
         device_id=partner, device_id_type=MESH,
     )
     swap.start()
     pending.append(swap)
-    pair[c] = y_ref[pl.ds(half * c, half)]
+    pair[:, c] = y_ref[pl.ds(half * c, half)]
     swap.wait_recv()
 
     def rows_of(r):
-        return jnp.concatenate([pair[0, r], pair[1, r]], axis=0)
+        return jnp.concatenate([pair[r, 0], pair[r, 1]], axis=0)
+
+    spread = exchange(ny, y, dev_y, lambda q: pair.at[pl.ds(per * q, per)], y_all.at[y])
+    y_all[y] = pair[pl.ds(per * y, per)]
 
     total = jnp.zeros((LANES, LANES), jnp.float32)
     for r in range(0, half, 2):
@@ -455,14 +458,23 @@
     merged = matmul_t(matmul(joined, gram), joined)
     basis = matmul(rounded(top_rows([(merged, 0)])[0]), joined).astype(jnp.bfloat16)
 
-    for r in range(0, half, 2):
-        wide = jnp.concatenate([rows_of(r), rows_of(r + 1)], axis=1)
-        modes = dot(basis, wide, ((1,), (0,))).astype(jnp.bfloat16)
-        a_own[r] = modes[:, :LANES]
-        a_own[r + 1] = modes[:, LANES:]
-    copies = exchange(ny, y, dev_y, lambda q: a_own.at[pl.ds(per * q, per)], a_all.at[y])
-    a_all[y] = a_own[pl.ds(per * y, per)]
+    basis_all[y] = basis
+    copies = exchange(ny, y, dev_y, lambda q: basis_all.at[y], basis_all.at[y])
+    used = basis.astype(jnp.float32)
+    below = jnp.zeros((LANES - RANK, LANES), jnp.float32)
+    block = matmul_t(matmul(used, gram), jnp.concatenate([used, below], axis=0))
+    folded = block[:8]
+    for i in range(1, RANK // 8):
+        folded = folded + pltpu.roll(block[8 * i : 8 * i + 8], RANK * i, 1)
+    own_blocks[y] = folded
+    block_copies = exchange(ny, y, dev_y, lambda q: own_blocks.at[y], own_blocks.at[y])
     arrive(copies)
+    arrive(spread)
+    for b in range(ny):
+        weights = basis_all[b]
+        for r in range(per):
+            snaps = jnp.concatenate([y_all[b, r, 0], y_all[b, r, 1]], axis=0)
+            a_all[b, r] = dot(weights, snaps, ((1,), (0,))).astype(jnp.bfloat16)
 
     stacked = jnp.concatenate(
         [
@@ -501,21 +513,9 @@
 
     pieces = []
     for b in range(ny):
-        window = lane_window(full[RANK * b : RANK * b + RANK], RANK * b)
-        pieces.append(jnp.where(lane < RANK * near, window, 0.0))
-    extra = jnp.zeros((RANK, LANES), jnp.float32)
-    for q in range(near):
-        col = RANK * (q + near)
-        tile, inner = col // LANES, col % LANES
-        block = full[RANK * q : RANK * q + RANK, LANES * tile : LANES * tile + LANES]
-        shift = (RANK * q - inner) % LANES
-        if shift:
-            block = pltpu.roll(block, shift, 1)
-        extra = jnp.where((lane >= RANK * q) & (lane < RANK * q + RANK), block, extra)
-    pieces.append(extra)
-    tall = g2_part.shape[0] * g2_part.shape[1] - RANK * (ny + 1)
-    if tall:
-        pieces.append(jnp.zeros((tall, LANES), jnp.float32))
+        window = lane_window(full[RANK * b : RANK * b + RANK], RANK * (b + 1) % width)
+        valid = RANK * (near if b < near else near - 1)
+        pieces.append(jnp.where(lane < valid, window, 0.0))
     g2_part[...] = jnp.concatenate(pieces, axis=0).reshape(g2_part.shape)
     copies = exchange(nxc, p, dev_xc, lambda q: g2_part.at[q], g2_rs.at[p])
     g2_rs[p] = g2_part[p]
@@ -554,27 +554,30 @@
 
     zero = jnp.zeros((RANK, LANES), jnp.float32)
     upper = [[None] * tiles for _ in range(ny)]
-    extra = flat[RANK * ny : RANK * ny + RANK]
+    arrive(block_copies)
     for b in range(ny):
         block = flat[RANK * b : RANK * b + RANK]
-        block = jnp.where(lane < RANK, 0.5 * block, block)
+        folded = own_blocks[b]
         for tile in range(tiles):
             got = zero
-            for off in range(near):
+            for off in range(near + 1 if b < near else near):
                 col = (RANK * (b + off)) % width
                 if col // LANES != tile:
                     continue
                 inner = col % LANES
-                shift = (inner - RANK * off) % LANES
-                moved = pltpu.roll(block, shift, 1) if shift else block
+                if off == 0:
+                    moved = 0.5 * jnp.concatenate(
+                        [
+                            pltpu.roll(folded, (inner - RANK * i) % LANES, 1)
+                            if (inner - RANK * i) % LANES else folded
+                            for i in range(RANK // 8)
+                        ],
+                        axis=0,
+                    )
+                else:
+                    shift = (inner - RANK * (off - 1)) % LANES
+                    moved = pltpu.roll(block, shift, 1) if shift else block
                 got = jnp.where((lane >= inner) & (lane < inner + RANK), moved, got)
-            if b < near:
-                col = RANK * (b + near)
-                if col // LANES == tile:
-                    inner = col % LANES
-                    shift = (inner - RANK * b) % LANES
-                    moved = pltpu.roll(extra, shift, 1) if shift else extra
-                    got = jnp.where((lane >= inner) & (lane < inner + RANK), moved, got)
             upper[b][tile] = got
     per_tile = LANES // RANK
 
@@ -591,12 +594,12 @@
         give(half_own.at[c])
         halves = [half_own[0], half_own[1]]
 
-        def spread(a, b):
+        def beside(a, b):
             return jnp.concatenate([a, b, zeros64], axis=0)
 
         pad = jnp.zeros((RANK, LANES), jnp.float32)
-        first = spread(halves[0], pad)
-        second = spread(pad, halves[1])
+        first = beside(halves[0], pad)
+        second = beside(pad, halves[1])
         upper_part = matmul_t(matmul(first, sym[0][1]), second)
         last = (
             matmul_t(matmul(first, sym[0][0]), first)
@@ -669,9 +672,8 @@
     packed = jnp.sum(coef_z[...].astype(jnp.float32), axis=0)
     solved = jnp.concatenate([packed[:, :64], packed[:, 64:]], axis=0).astype(jnp.bfloat16)
 
-    solved_t = solved.T
-    for r in range(height):
-        out_ref[r] = dot(solved_t, f_all[r], ((1,), (0,))).astype(jnp.bfloat16)
+    solved_out[...] = solved
+    f_out[...] = f_all[...]
     for copy in pending:
         copy.wait_send()
 
@@ -685,8 +687,7 @@
         padded += unit
     half = padded // 2
     per = half // ny
-    tall = RANK * (ny + 1)
-    piece2 = -(-tall // (8 * nxc)) * 8
+    piece2 = RANK * ny // nxc
     f32, bf16 = jnp.float32, jnp.bfloat16
     vm = pltpu.VMEM
     reach = -(-(ROW_BASE + height + PASSES) // 8) * 8
@@ -695,9 +696,12 @@
     sems = max(8, nxc, ny, nz)
     return pl.pallas_call(
         functools.partial(merge_kernel, ny, nx, nz),
-        out_shape=jax.ShapeDtypeStruct(residuals.shape, bf16),
+        out_shape=(
+            jax.ShapeDtypeStruct((RANK, 64), bf16),
+            jax.ShapeDtypeStruct((padded, RANK, LANES), bf16),
+        ),
         in_specs=[pl.BlockSpec(memory_space=pl.ANY), pl.BlockSpec(memory_space=pltpu.VMEM)],
-        out_specs=pl.BlockSpec(memory_space=pltpu.VMEM),
+        out_specs=(pl.BlockSpec(memory_space=pltpu.VMEM),) * 2,
         scratch_shapes=[
             vm(residuals.shape, bf16),
             vm((64, reach + 8, LANES), f32),
@@ -720,12 +724,14 @@
             vm((2, 3, 4, 8, LANES), bf16),
             vm((2, height, LANES), f32),
             vm((2, 3, 8, LANES), f32),
-            vm((2, half, 64, LANES), bf16),
+            vm((half, 2, 64, LANES), bf16),
+            vm((ny, per, 2, 64, LANES), bf16),
+            vm((ny, RANK, LANES), bf16),
+            vm((ny, 8, LANES), f32),
             vm((nxc, LANES // nxc, LANES), f32),
             vm((nxc, LANES // nxc, LANES), f32),
             vm((nz, LANES // nxc, LANES), f32),
             vm((nxc, LANES // nxc, LANES), f32),
-            vm((half, RANK, LANES), bf16),
             vm((ny, per, RANK, LANES), bf16),
             vm((nxc, piece2, LANES), f32),
             vm((nxc, piece2, LANES), f32),
@@ -737,8 +743,8 @@
             vm((nz, 16, LANES), bf16),
             vm((2, RANK, LANES), f32),
             vm((2, RANK, LANES), f32),
-            pltpu.SemaphoreType.DMA((20, sems)),
-            pltpu.SemaphoreType.DMA((20, sems)),
+            pltpu.SemaphoreType.DMA((22, sems)),
+            pltpu.SemaphoreType.DMA((22, sems)),
             pltpu.SemaphoreType.DMA,
         ],
         compiler_params=pltpu.CompilerParams(collective_id=0, has_side_effects=True),
@@ -746,11 +752,33 @@
     )(residuals, diffusivity)
 
 
+def project_kernel(solved_ref, modes_ref, out_ref):
+    solved = solved_ref[...].T
+    for r in range(out_ref.shape[0]):
+        out_ref[r] = dot(solved, modes_ref[r], ((1,), (0,))).astype(jnp.bfloat16)
+
+
+def project_call(solved, modes, height):
+    block = max(n for n in range(1, 10) if height % n == 0)
+    return pl.pallas_call(
+        project_kernel,
+        grid=(height // block,),
+        out_shape=jax.ShapeDtypeStruct((height, 64, LANES), jnp.bfloat16),
+        in_specs=[
+            pl.BlockSpec((RANK, 64), lambda i: (0, 0)),
+            pl.BlockSpec((block, RANK, LANES), lambda i: (i, 0, 0)),
+        ],
+        out_specs=pl.BlockSpec((block, 64, LANES), lambda i: (i, 0, 0)),
+        name="project",
+    )(solved, modes)
+
+
 def shards(residuals, diffusivity):
-    projected = merge_call(
+    solved, modes = merge_call(
         residuals.transpose(1, 0, 2), diffusivity,
         lax.axis_size("tm") // 2, lax.axis_size("lat"), lax.axis_size("lon"),
     )
+    projected = project_call(solved, modes, residuals.shape[1])
     return projected.transpose(1, 0, 2)
 
 

time: 124 us -> 123 us (level)
  local copies, waits for them, and re-layouts: 2.03 us -> 0 us
    unnamed x1 -> x0, local copies, waits for them, and re-layouts: 2.03 us -> none
    pallas_call x1 -> x2, Pallas kernels: 122 us -> 123 us  [the longest x1 119 us: merge_call(): pl.pallas_call(functools.partial(merge_kernel, ny, nx, nz), out_shape=(ja...]
where the time goes in v5:
time: 123 us
  Pallas kernels  123 us (100%)
    pallas_call x1, Pallas kernels, merge_call(): pl.pallas_call(functools.partial(merge_kernel, ny, nx, nz), out_shape=(ja...  119 us
    pallas_call x1, Pallas kernels, project_call(): pl.pallas_call(project_kernel, grid=(height // block,), out_shape=jax.Sha...  4.15 us

profile of v5, /device:TPU:1, one launch (start us, length us, event | category | flops | bytes accessed | tf_op | source)
XLA Modules:
  0.0 122.9 jit_solution(11557945094324236861)
XLA Ops:
  0.0 118.7 %merge.1 = (bf16[32,64]{1,0:T(8,128)(2,1)}, bf16[48,32,128]{2,1,0:T(8,128)(2,1)}) custom-call(bf16[45,64,128]{2,1,0:T(8,128)(2,1)} %bitcast.2, f32[45,128]{1,0:T(8,128)} %dif_ref.1), custom_call_target="tpu_custom_call" | custom-call | tf_op jit(solution)/shard_map/merge/pallas_call | solution.py:697
  118.7 4.2 %project.1 = bf16[45,64,128]{2,1,0:T(8,128)(2,1)} custom-call(bf16[32,64]{1,0:T(8,128)(2,1)} %get-tuple-element.7.solved_ref, bf16[48,32,128]{2,1,0:T(8,128)(2,1)} %get-tuple-element.8.modes_ref), custom_call_target="tpu_custom_call" | custom-call | tf_op jit(solution)/shard_map/project/pallas_call | solution.py:763

commit v6 on v5

--- a/solution.py
+++ b/solution.py
@@ -246,19 +246,72 @@
         pending.append(copy)
 
     for side, dx in ((0, -1), (1, 1)):
+        for dz in (-1, 0, 1):
+            pass_on(dif_edge.at[side], got_dif_edge.at[side, dz + 1], dx, dz)
+    for dz in (-1, 1):
+        pass_on(dif_ref, got_dif.at[(dz + 1) // 2], 0, dz)
+    early = len(halo)
+    for side, dx in ((0, -1), (1, 1)):
         for dz in (-1, 1):
             pass_on(pack_edge.at[side], got_edge.at[side, dz + 1], dx, dz)
-            pass_on(dif_edge.at[side], got_dif_edge.at[side, dz + 1], dx, dz)
+        pass_on(edge_rows.at[side], got_rows.at[side], dx, 0)
         pass_on(pack_edge.at[side], got_edge.at[side, 1], dx, 0)
-        pass_on(dif_edge.at[side], got_dif_edge.at[side, 1], dx, 0)
-        pass_on(edge_rows.at[side], got_rows.at[side], dx, 0)
     for dz in (-1, 1):
         pass_on(pack, got_pack.at[(dz + 1) // 2], 0, dz)
-        pass_on(dif_ref, got_dif.at[(dz + 1) // 2], 0, dz)
-    for copy in halo:
+    has_north, has_south = x > 0, x < nx - 1
+    for copy in halo[:early]:
         copy.wait_recv()
 
-    has_north, has_south = x > 0, x < nx - 1
+    wide = height + 2 * edge
+
+    def tall_of(middle, k):
+        north = jnp.where(has_north, got_dif_edge[1, k, pl.ds(0, edge), :], 0.0)
+        south = jnp.where(has_south, got_dif_edge[0, k, pl.ds(0, edge), :], 0.0)
+        return jnp.concatenate([north, middle, south], axis=0)
+
+    own_d = tall_of(dif_ref[...], 1)
+    west_d = tall_of(got_dif[1], 2)
+    east_d = tall_of(got_dif[0], 0)
+    lane_w = lax.broadcasted_iota(jnp.int32, (wide, LANES), 1)
+    row_w = lax.broadcasted_iota(jnp.int32, (wide, LANES), 0)
+    inside = ((row_w >= edge) | has_north) & ((row_w < height + edge) | has_south)
+
+    def five(center, left, right):
+        zero_row = jnp.zeros((1, LANES), jnp.float32)
+        up = jnp.concatenate([zero_row, center[:-1]], axis=0)
+        down = jnp.concatenate([center[1:], zero_row], axis=0)
+        ks = [jnp.where(inside, 0.5 * (center + v), 0.0) for v in (up, down, left, right)]
+        return [1.0 - (ks[0] + ks[1] + ks[2] + ks[3])] + ks
+
+    left = jnp.where(lane_w == 0, pltpu.roll(west_d, 1, 1), pltpu.roll(own_d, 1, 1))
+    right = jnp.where(lane_w == LANES - 1, pltpu.roll(east_d, LANES - 1, 1), pltpu.roll(own_d, LANES - 1, 1))
+    main = five(own_d, left, right)
+    for k in range(5):
+        coef_0[k, pl.ds(base - edge, wide), :] = main[k]
+
+    def turn(j, carry):
+        for k in range(5):
+            coef_m[j, k, pl.ds(base - edge, wide), :] = pltpu.roll(
+                coef_0[k, pl.ds(base - edge, wide), :], 8 * j + 4, 1
+            )
+        return carry
+
+    lax.fori_loop(0, 16, turn, 0, unroll=2)
+    for which, (first_d, second_d) in enumerate(((west_d, own_d), (own_d, east_d))):
+        strip = jnp.where(
+            lane_w < 4,
+            pltpu.roll(first_d, 4, 1),
+            jnp.where(lane_w < 8, pltpu.roll(second_d, 4, 1), 0.0),
+        )
+        for shift in (8, 16, 32, 64):
+            strip = strip + pltpu.roll(strip, shift, 1)
+        ks = five(strip, pltpu.roll(strip, 1, 1), pltpu.roll(strip, LANES - 1, 1))
+        for k in range(5):
+            coef_s[which, k, pl.ds(base - edge, wide), :] = ks[k]
+
+    for copy in halo[early:]:
+        copy.wait_recv()
+
     for side, first, there in ((1, base - edge, has_north), (0, base + height, has_south)):
         for e in range(edge):
             row = got_rows[side, e].astype(jnp.float32)
@@ -284,53 +337,6 @@
             )
             west_a[g, pl.ds(first, edge), :] = seam(own, from_west, edge, False)
             east_a[g, pl.ds(first, edge), :] = seam(own, from_east, edge, True)
-
-    wide = height + 2 * edge
-
-    def tall_of(middle, k):
-        north = jnp.where(has_north, got_dif_edge[1, k, pl.ds(0, edge), :], 0.0)
-        south = jnp.where(has_south, got_dif_edge[0, k, pl.ds(0, edge), :], 0.0)
-        return jnp.concatenate([north, middle, south], axis=0)
-
-    own_d = tall_of(dif_ref[...], 1)
-    west_d = tall_of(got_dif[1], 2)
-    east_d = tall_of(got_dif[0], 0)
-    lane_w = lax.broadcasted_iota(jnp.int32, (wide, LANES), 1)
-    row_w = lax.broadcasted_iota(jnp.int32, (wide, LANES), 0)
-    inside = ((row_w >= edge) | has_north) & ((row_w < height + edge) | has_south)
-
-    def five(center, left, right):
-        zero_row = jnp.zeros((1, LANES), jnp.float32)
-        up = jnp.concatenate([zero_row, center[:-1]], axis=0)
-        down = jnp.concatenate([center[1:], zero_row], axis=0)
-        ks = [jnp.where(inside, 0.5 * (center + v), 0.0) for v in (up, down, left, right)]
-        return [1.0 - (ks[0] + ks[1] + ks[2] + ks[3])] + ks
-
-    left = jnp.where(lane_w == 0, pltpu.roll(west_d, 1, 1), pltpu.roll(own_d, 1, 1))
-    right = jnp.where(lane_w == LANES - 1, pltpu.roll(east_d, LANES - 1, 1), pltpu.roll(own_d, LANES - 1, 1))
-    main = five(own_d, left, right)
-    for k in range(5):
-        coef_0[k, pl.ds(base - edge, wide), :] = main[k]
-
-    def turn(j, carry):
-        for k in range(5):
-            coef_m[j, k, pl.ds(base - edge, wide), :] = pltpu.roll(
-                coef_0[k, pl.ds(base - edge, wide), :], 8 * j + 4, 1
-            )
-        return carry
-
-    lax.fori_loop(0, 16, turn, 0, unroll=2)
-    for which, (first_d, second_d) in enumerate(((west_d, own_d), (own_d, east_d))):
-        strip = jnp.where(
-            lane_w < 4,
-            pltpu.roll(first_d, 4, 1),
-            jnp.where(lane_w < 8, pltpu.roll(second_d, 4, 1), 0.0),
-        )
-        for shift in (8, 16, 32, 64):
-            strip = strip + pltpu.roll(strip, shift, 1)
-        ks = five(strip, pltpu.roll(strip, 1, 1), pltpu.roll(strip, LANES - 1, 1))
-        for k in range(5):
-            coef_s[which, k, pl.ds(base - edge, wide), :] = ks[k]
 
     def weighted_sum(c, center, north, south, left, right):
         return center * c[0] + north * c[1] + south * c[2] + left * c[3] + right * c[4]
@@ -759,16 +765,11 @@
 
 
 def project_call(solved, modes, height):
-    block = max(n for n in range(1, 10) if height % n == 0)
     return pl.pallas_call(
         project_kernel,
-        grid=(height // block,),
         out_shape=jax.ShapeDtypeStruct((height, 64, LANES), jnp.bfloat16),
-        in_specs=[
-            pl.BlockSpec((RANK, 64), lambda i: (0, 0)),
-            pl.BlockSpec((block, RANK, LANES), lambda i: (i, 0, 0)),
-        ],
-        out_specs=pl.BlockSpec((block, 64, LANES), lambda i: (i, 0, 0)),
+        in_specs=[pl.BlockSpec(memory_space=pltpu.VMEM)] * 2,
+        out_specs=pl.BlockSpec(memory_space=pltpu.VMEM),
         name="project",
     )(solved, modes)
 

time: 123 us -> 121 us (0.984)
  Pallas kernels: 123 us -> 121 us
    pallas_call x1, Pallas kernels: 4.15 us -> 2.27 us  [project_call(): pl.pallas_call(project_kernel, out_shape=jax.ShapeDtypeStruct((height, 64...]
where the time goes in v6:
time: 121 us
  Pallas kernels  121 us (100%)
    pallas_call x1, Pallas kernels, merge_call(): pl.pallas_call(functools.partial(merge_kernel, ny, nx, nz), out_shape=(ja...  119 us

profile of v6, /device:TPU:1, one launch (start us, length us, event | category | flops | bytes accessed | tf_op | source)
XLA Modules:
  0.0 120.9 jit_solution(16682936552170650955)
XLA Ops:
  0.0 118.7 %merge.1 = (bf16[32,64]{1,0:T(8,128)(2,1)}, bf16[48,32,128]{2,1,0:T(8,128)(2,1)}) custom-call(bf16[45,64,128]{2,1,0:T(8,128)(2,1)} %bitcast.2, f32[45,128]{1,0:T(8,128)} %dif_ref.1), custom_call_target="tpu_custom_call" | custom-call | tf_op jit(solution)/shard_map/merge/pallas_call | solution.py:703
  118.7 2.3 %project.1 = bf16[45,64,128]{2,1,0:T(8,128)(2,1)} custom-call(bf16[32,64]{1,0:T(8,128)(2,1)} %get-tuple-element.7.solved_ref, bf16[48,32,128]{2,1,0:T(8,128)(2,1)} %get-tuple-element.8.modes_ref), custom_call_target="tpu_custom_call" | custom-call | tf_op jit(solution)/shard_map/project/pallas_call | solution.py:768

commit v7 on v6

--- a/solution.py
+++ b/solution.py
@@ -111,19 +111,6 @@
     return lax.fori_loop(0, POWER, body, start)
 
 
-def merge_pairs(grams):
-    problems = [(g, side) for g in grams for side in (0, 1)]
-    tops = top_rows(problems)
-    zeros = jnp.zeros((64, LANES), jnp.float32)
-    joined = [
-        jnp.concatenate([rounded(tops[2 * i]), rounded(tops[2 * i + 1]), zeros], axis=0)
-        for i in range(len(grams))
-    ]
-    merged = [matmul_t(matmul(j, g), j) for j, g in zip(joined, grams)]
-    second = top_rows([(m, 0) for m in merged])
-    return [matmul(rounded(p), j) for p, j in zip(second, joined)]
-
-
 def order_of(n):
     return sorted(range(1, n), key=lambda d: -min(d, n - d))
 
@@ -134,7 +121,7 @@
     got_rows, got_pack, got_edge, got_dif, got_dif_edge,
     pair, y_all, basis_all, own_blocks, gram_part, gram_rs, gram_z, gram_ag,
     a_all, g2_part, g2_rs, g2_y, g2_z, g2_ag,
-    f_all, coef_x, coef_z, top_own, half_own,
+    f_all, coef_x, coef_z, top_own, half_own, pair_own,
     send, recv, load_sem,
 ):
     t, x, z = lax.axis_index("tm"), lax.axis_index("lat"), lax.axis_index("lon")
@@ -409,13 +396,13 @@
     for i in range(height, y_ref.shape[0]):
         y_ref[i] = jnp.zeros((64, LANES), jnp.bfloat16)
 
-    def give(block):
+    def give(block, peer):
         at = stage_count[0]
         stage_count[0] += 1
         copy = pltpu.make_async_remote_copy(
             src_ref=block, dst_ref=block,
             send_sem=send.at[at, 0], recv_sem=recv.at[at, 0],
-            device_id=partner, device_id_type=MESH,
+            device_id=peer, device_id_type=MESH,
         )
         copy.start()
         pending.append(copy)
@@ -456,13 +443,17 @@
     arrive(copies)
     gram = gram_ag[...].reshape(LANES, LANES)
 
-    own_gram = jnp.where(c == 0, gram[:64], pltpu.roll(gram[64:], 64, 1))
     zeros64 = jnp.zeros((64, LANES), jnp.float32)
-    top_own[c] = rounded(top_rows([(jnp.concatenate([own_gram, zeros64], axis=0), 0)])[0])
-    give(top_own.at[c])
-    joined = jnp.concatenate([top_own[0], pltpu.roll(top_own[1], 64, 1), zeros64], axis=0)
-    merged = matmul_t(matmul(joined, gram), joined)
-    basis = matmul(rounded(top_rows([(merged, 0)])[0]), joined).astype(jnp.bfloat16)
+
+    def merge_shared(both, side, tops, peer):
+        own = jnp.where(side == 0, both[:64], pltpu.roll(both[64:], 64, 1))
+        tops[side] = rounded(top_rows([(jnp.concatenate([own, zeros64], axis=0), 0)])[0])
+        give(tops.at[side], peer)
+        joined = jnp.concatenate([tops[0], pltpu.roll(tops[1], 64, 1), zeros64], axis=0)
+        merged = matmul_t(matmul(joined, both), joined)
+        return matmul(rounded(top_rows([(merged, 0)])[0]), joined)
+
+    basis = merge_shared(gram, c, top_own, partner).astype(jnp.bfloat16)
 
     basis_all[y] = basis
     copies = exchange(ny, y, dev_y, lambda q: basis_all.at[y], basis_all.at[y])
@@ -596,8 +587,11 @@
     sym = [[up[i][j] + up[j][i].T for j in range(tiles)] for i in range(tiles)]
 
     if tiles == 2:
-        half_own[c] = rounded(merge_pairs([jnp.where(c == 0, sym[0][0], sym[1][1])])[0])
-        give(half_own.at[c])
+        side = lax.rem(x, 2)
+        along = (t, x + 1 - 2 * side, z)
+        tile = jnp.where(c == 0, sym[0][0], sym[1][1])
+        half_own[c] = rounded(merge_shared(tile, side, pair_own, along))
+        give(half_own.at[c], partner)
         halves = [half_own[0], half_own[1]]
 
         def beside(a, b):
@@ -749,8 +743,9 @@
             vm((nz, 16, LANES), bf16),
             vm((2, RANK, LANES), f32),
             vm((2, RANK, LANES), f32),
-            pltpu.SemaphoreType.DMA((22, sems)),
-            pltpu.SemaphoreType.DMA((22, sems)),
+            vm((2, RANK, LANES), f32),
+            pltpu.SemaphoreType.DMA((23, sems)),
+            pltpu.SemaphoreType.DMA((23, sems)),
             pltpu.SemaphoreType.DMA,
         ],
         compiler_params=pltpu.CompilerParams(collective_id=0, has_side_effects=True),

time: 121 us -> 121 us (level); the launches traced: 121 us -> 119 us
  Pallas kernels: 121 us -> 119 us
    pallas_call x1, Pallas kernels: 119 us -> 117 us  [merge_call(): pl.pallas_call(functools.partial(merge_kernel, ny, nx, nz), out_shape=(ja...]
where the time goes in v7:
time: 121 us; the launch traced here: 119 us
  Pallas kernels  119 us (98%)
    pallas_call x1, Pallas kernels, merge_call(): pl.pallas_call(functools.partial(merge_kernel, ny, nx, nz), out_shape=(ja...  117 us

profile of v7, /device:TPU:1, one launch (start us, length us, event | category | flops | bytes accessed | tf_op | source)
XLA Modules:
  0.0 119.2 jit_solution(16842324827950873067)
XLA Ops:
  0.0 116.9 %merge.1 = (bf16[32,64]{1,0:T(8,128)(2,1)}, bf16[48,32,128]{2,1,0:T(8,128)(2,1)}) custom-call(bf16[45,64,128]{2,1,0:T(8,128)(2,1)} %bitcast.2, f32[45,128]{1,0:T(8,128)} %dif_ref.1), custom_call_target="tpu_custom_call" | custom-call | tf_op jit(solution)/shard_map/merge/pallas_call | solution.py:697
  117.0 2.3 %project.1 = bf16[45,64,128]{2,1,0:T(8,128)(2,1)} custom-call(bf16[32,64]{1,0:T(8,128)(2,1)} %get-tuple-element.7.solved_ref, bf16[48,32,128]{2,1,0:T(8,128)(2,1)} %get-tuple-element.8.modes_ref), custom_call_target="tpu_custom_call" | custom-call | tf_op jit(solution)/shard_map/project/pallas_call | solution.py:763
